TPU v7x, 32 devices: a whole 2x2x4 slice. The times are simulated.
32 devices in a mesh: shard: 4 (over z), context: 2 (over x), tensor: 4 (over y, core).
Axes of the slice: x: 2, y: 2, z: 4, core: 2. Of those that a mesh axis runs over, the one named last changes fastest.
Arguments:
- hidden_in: bfloat16 [4, 2048, 1536], P('shard', 'context'), may hold values from -6 to 6
- norm_gain: float32 [1536], replicated, may hold values from 0.5 to 1.5
- w_in_zx: bfloat16 [1536, 2, 3072], P('shard', None, 'tensor'), may hold values from -0.15625 to 0.15625
- w_in_bc: bfloat16 [1536, 256], P('shard'), may hold values from -0.15625 to 0.15625
- w_in_dt: bfloat16 [1536, 48], P('shard', 'tensor'), may hold values from -0.15625 to 0.15625
- conv_x: float32 [5, 3072], P(None, 'tensor'), may hold values from -3 to 3
- conv_bc: float32 [5, 256], replicated, may hold values from -3 to 3
- dt_bias: float32 [48], P('tensor'), may hold values from -6 to -2.5
- a_log: float32 [48], P('tensor'), may hold values from -1 to 1.5
- d_skip: float32 [48], P('tensor'), may hold values from 0.5 to 1.5
- out_gain: float32 [3072], P('tensor'), may hold values from 0.5 to 1.5
- w_out: bfloat16 [3072, 1536], P('tensor', 'shard'), may hold values from -0.109375 to 0.109375
- cotangent: bfloat16 [4, 2048, 1536], P('shard', 'context'), may hold values from -6 to 6
Outputs:
- out: bfloat16 [4, 2048, 1536], P('shard', 'context')
- grad_in: float32 [4, 2048, 1536], P('shard', 'context')
- grad_norm_gain: float32 [1536], replicated
- grad_w_in_zx: float32 [1536, 2, 3072], P(('shard', 'context'), None, 'tensor')
- grad_w_in_bc: float32 [1536, 256], P(('shard', 'context'))
- grad_w_in_dt: float32 [1536, 48], P(('shard', 'context'), 'tensor')
- grad_conv_x: float32 [5, 3072], P(None, 'tensor')
- grad_conv_bc: float32 [5, 256], replicated
- grad_dt_bias: float32 [48], P('tensor')
- grad_a_log: float32 [48], P('tensor')
- grad_d_skip: float32 [48], P('tensor')
- grad_out_gain: float32 [3072], P('tensor')
- grad_w_out: float32 [3072, 1536], P('tensor', ('shard', 'context'))
- rms_stream: float32 [], replicated
- rms_mixer: float32 [], replicated
All inputs are finite; a program needn't handle non-finite values.
Results may differ from a plain program's by a relative error of at most 0.012.
Values may be sent and summed in bfloat16 or wider, within the bound.
No kernel may reach another device: no remote copies, remote signals or barrier semaphores. Data moves between devices by JAX's collectives and lax.ppermute only.
A program may use at most 192 MiB of HBM per device.

v0:
```python
import jax
import jax.numpy as jnp
from jax import lax
from jax.sharding import PartitionSpec as P

CH = 256


EPSILON = 1e-05
PRECISE = lax.Precision.HIGHEST


def shifted(array, axis, by):
    length = lax.axis_size(axis)
    pairs = [(i, i + by) for i in range(length) if 0 <= i + by < length]
    return lax.ppermute(array, axis, pairs)


def carried_in(array, axis, combine, identity, reverse):
    length, place = (lax.axis_size(axis), lax.axis_index(axis))
    everything = jax.tree.map(lambda part: lax.all_gather(part, axis), array)
    start = jax.tree.map(
        lambda part, zero: jnp.broadcast_to(jnp.asarray(zero, part.dtype), part.shape),
        array,
        identity,
    )

    def hop(k, before):
        at = length - 1 - k if reverse else k
        reached = at > place if reverse else at < place
        new = combine(before, jax.tree.map(lambda part: part[at], everything))
        return jax.tree.map(lambda a, b: jnp.where(reached, a, b), new, before)

    return lax.fori_loop(0, length, hop, start)


def combine_states(earlier, nearer):
    return (earlier[0] * nearer[0], nearer[0][..., None, None] * earlier[1] + nearer[1])


def silu_grad(values, sigmoid_val):
    return sigmoid_val * (1.0 + values * (1.0 - sigmoid_val))


def contract_rows(left_op, right_op):
    return lax.dot_general(
        left_op, right_op, (((0,), (0,)), ((), ())), preferred_element_type=jnp.float32
    )


def contract_cols(left_op, right_op):
    return lax.dot_general(
        left_op, right_op, (((1,), (1,)), ((), ())), preferred_element_type=jnp.float32
    )


def reverse_cumsum(values, axis_num):
    return jnp.flip(jnp.cumsum(jnp.flip(values, axis_num), axis=axis_num), axis_num)


def advance(running, element):
    return (element[0][..., None, None] * running + element[1], running)


def retreat(running, element):
    return (element[1] + element[0][..., None, None] * running, running)


def on_device(
    hidden_in,
    norm_gain,
    w_in_zx,
    w_in_bc,
    w_in_dt,
    conv_x,
    conv_bc,
    dt_bias,
    a_log,
    d_skip,
    out_gain,
    w_out,
    cotangent,
):
    seq_count, local_len, model_dim = hidden_in.shape
    inner_dev = w_in_zx.shape[2]
    heads_dev = w_in_dt.shape[1]
    head_dim = inner_dev // heads_dev
    state_dim = w_in_bc.shape[1] // 2
    tap_count = conv_x.shape[0] - 1
    inner_all = inner_dev * lax.axis_size("tensor")
    block_len = CH
    block_count = local_len // block_len
    row_count = seq_count * local_len
    channels = inner_dev + 2 * state_dim
    zx_full, bc_full, dt_full, out_full = (
        lax.all_gather(w_in_zx, "shard", axis=0, tiled=True),
        lax.all_gather(w_in_bc, "shard", axis=0, tiled=True),
        lax.all_gather(w_in_dt, "shard", axis=0, tiled=True),
        lax.all_gather(w_out, "shard", axis=1, tiled=True),
    )
    zx_mat = zx_full.reshape(model_dim, 2 * inner_dev)
    stream_in = hidden_in.reshape(row_count, model_dim).astype(jnp.float32)
    scale_in = lax.rsqrt(jnp.mean(stream_in * stream_in, axis=-1, keepdims=True) + EPSILON)
    normed = (stream_in * scale_in * norm_gain).astype(jnp.bfloat16)
    zx_val = jnp.dot(normed, zx_mat, preferred_element_type=jnp.float32)
    gate_val = zx_val[:, :inner_dev]
    bc_val = jnp.dot(normed, bc_full, preferred_element_type=jnp.float32)
    dt_raw = jnp.dot(normed, dt_full, preferred_element_type=jnp.float32)
    pre_conv = jnp.concatenate([zx_val[:, inner_dev:], bc_val], axis=-1).reshape(
        seq_count, local_len, channels
    )
    prev_rows = shifted(pre_conv[:, local_len - tap_count + 1 :], "context", 1)
    padded = jnp.concatenate([prev_rows, pre_conv], axis=1)
    conv_all = jnp.concatenate([conv_x, conv_bc], axis=1)
    conv_out = conv_all[tap_count] + conv_all[0] * padded[:, 0:local_len]
    for tap_idx in range(1, tap_count):
        conv_out = conv_out + conv_all[tap_idx] * padded[:, tap_idx : tap_idx + local_len]
    sig_conv = jax.nn.sigmoid(conv_out)
    activated = (conv_out * sig_conv).astype(jnp.bfloat16)
    xa_blk = activated[..., :inner_dev].reshape(
        seq_count, block_count, block_len, heads_dev, head_dim
    )
    bm_blk = activated[..., inner_dev : inner_dev + state_dim].reshape(
        seq_count, block_count, block_len, state_dim
    )
    cm_blk = activated[..., inner_dev + state_dim :].reshape(
        seq_count, block_count, block_len, state_dim
    )
    xa_f = xa_blk.astype(jnp.float32)
    bm_f = bm_blk.astype(jnp.float32)
    cm_f = cm_blk.astype(jnp.float32)
    dt_pre = dt_raw + dt_bias
    dt_val = jax.nn.softplus(dt_pre)
    rate_neg = -jnp.exp(a_log)
    dt_q = dt_val.reshape(seq_count, block_count, block_len, heads_dev)
    log_q = (dt_val * rate_neg).reshape(seq_count, block_count, block_len, heads_dev)
    cum_q = jnp.cumsum(log_q, axis=2)
    block_log = cum_q[:, :, -1]
    cum_t = jnp.swapaxes(cum_q, 2, 3)
    dt_t = jnp.swapaxes(dt_q, 2, 3)
    positions = jnp.arange(block_len)
    lower_mask = positions[:, None] >= positions[None, :]
    log_gap = cum_t[..., :, None] - cum_t[..., None, :]
    decay_mat = jnp.exp(jnp.where(lower_mask, log_gap, 0.0)) * lower_mask.astype(jnp.float32)
    scores = jnp.einsum("scin,scjn->scij", cm_blk, bm_blk, preferred_element_type=jnp.float32)
    weights_f = scores[:, :, None] * decay_mat * dt_t[..., None, :]
    weights_b = weights_f.astype(jnp.bfloat16)
    y_intra = jnp.einsum(
        "schij,scjhp->scihp", weights_b, xa_blk, preferred_element_type=jnp.float32
    )
    w_end = jnp.exp(block_log[:, :, None, :] - cum_q) * dt_q
    xw_val = (xa_f * w_end[..., None]).astype(jnp.bfloat16)
    state_add = jnp.einsum("scjn,scjhp->schnp", bm_blk, xw_val, preferred_element_type=jnp.float32)
    block_decay = jnp.exp(block_log)
    zero_state = jnp.zeros((seq_count, heads_dev, state_dim, head_dim), jnp.float32)
    end_local, start_local = lax.scan(
        advance, zero_state, (jnp.moveaxis(block_decay, 1, 0), jnp.moveaxis(state_add, 1, 0))
    )
    start_local = jnp.moveaxis(start_local, 0, 1)
    dev_decay = jnp.prod(block_decay, axis=1)
    _, in_state = carried_in(
        (dev_decay, end_local),
        "context",
        combine_states,
        (jnp.ones_like(dev_decay), jnp.zeros_like(end_local)),
        False,
    )
    before_dec = jnp.exp(jnp.cumsum(block_log, axis=1) - block_log)
    start_state = start_local + before_dec[..., None, None] * in_state[:, None]
    start_b = start_state.astype(jnp.bfloat16)
    cum_exp = jnp.exp(cum_q)
    cm_scaled = (cm_f[:, :, :, None, :] * cum_exp[..., None]).astype(jnp.bfloat16)
    y_inter = jnp.einsum(
        "scihn,schnp->scihp", cm_scaled, start_b, preferred_element_type=jnp.float32
    )
    y_ssd = (y_intra + y_inter + d_skip[:, None] * xa_f).reshape(row_count, inner_dev)
    sig_gate = jax.nn.sigmoid(gate_val)
    silu_gate = gate_val * sig_gate
    gated = y_ssd * silu_gate
    square_sum = lax.psum(jnp.sum(gated * gated, axis=-1), "tensor")
    scale_out = lax.rsqrt(square_sum / inner_all + EPSILON)[:, None]
    out_in = (gated * scale_out * out_gain).astype(jnp.bfloat16)
    mixed = lax.psum(jnp.dot(out_in, out_full, preferred_element_type=jnp.float32), "tensor")
    stream = stream_in + mixed
    stream_sq = jnp.sum(stream * stream)
    mixed_sq = jnp.sum(mixed * mixed)
    grad_rows = cotangent.reshape(row_count, model_dim)
    grad_stream = grad_rows.astype(jnp.float32)
    grad_wout = contract_rows(out_in, grad_rows)
    wout_share = lax.psum_scatter(grad_wout, ("shard", "context"), scatter_dimension=1, tiled=True)
    grad_on = contract_cols(grad_rows, out_full)
    grad_og = jnp.sum(grad_on * gated * scale_out, axis=0)
    grad_gn = grad_on * out_gain
    dot_sum = lax.psum(jnp.sum(grad_gn * gated, axis=-1), "tensor")
    grad_gated = scale_out * grad_gn - gated * scale_out**3 * (dot_sum / inner_all)[:, None]
    grad_y = (grad_gated * silu_gate).astype(jnp.bfloat16)
    grad_gate = (grad_gated * y_ssd * silu_grad(gate_val, sig_gate)).astype(jnp.bfloat16)
    grad_yb = grad_y.reshape(seq_count, block_count, block_len, heads_dev, head_dim)
    grad_yf = grad_yb.astype(jnp.float32)
    grad_wts = jnp.einsum("scihp,scjhp->schij", grad_yb, xa_blk, preferred_element_type=jnp.float32)
    grad_xa = (
        jnp.einsum("schij,scihp->scjhp", weights_b, grad_yb, preferred_element_type=jnp.float32)
        + d_skip[:, None] * grad_yf
    )
    grad_skip = jnp.sum(grad_yf * xa_f, axis=(0, 1, 2, 4))
    weighted = grad_wts * weights_f
    grad_cum_t = jnp.sum(weighted, axis=-1) - jnp.sum(weighted, axis=-2)
    grad_dt_t = jnp.sum(grad_wts * scores[:, :, None] * decay_mat, axis=-2)
    grad_scores = jnp.sum(grad_wts * decay_mat * dt_t[..., None, :], axis=2)
    grad_bm = jnp.einsum("scij,scin->scjn", grad_scores, cm_f, precision=PRECISE)
    grad_cm = jnp.einsum("scij,scjn->scin", grad_scores, bm_f, precision=PRECISE)
    grad_scaled = jnp.einsum(
        "scihp,schnp->scihn", grad_yb, start_b, preferred_element_type=jnp.float32
    )
    grad_cm = grad_cm + jnp.sum(grad_scaled * cum_exp[..., None], axis=3)
    grad_cum_q = (
        jnp.swapaxes(grad_cum_t, 2, 3)
        + jnp.sum(grad_scaled * cm_f[:, :, :, None, :], axis=-1) * cum_exp
    )
    grad_start = jnp.einsum(
        "scihn,scihp->schnp", cm_scaled, grad_yb, preferred_element_type=jnp.float32
    )
    gin_local, after_local = lax.scan(
        retreat,
        zero_state,
        (jnp.moveaxis(block_decay, 1, 0), jnp.moveaxis(grad_start, 1, 0)),
        reverse=True,
    )
    after_local = jnp.moveaxis(after_local, 0, 1)
    _, grad_end = carried_in(
        (dev_decay, gin_local),
        "context",
        combine_states,
        (jnp.ones_like(dev_decay), jnp.zeros_like(gin_local)),
        True,
    )
    after_dec = jnp.exp(jnp.sum(block_log, axis=1, keepdims=True) - jnp.cumsum(block_log, axis=1))
    grad_after = after_local + after_dec[..., None, None] * grad_end[:, None]
    grad_lam = block_decay * jnp.sum(grad_after * start_state, axis=(-2, -1))
    grad_after_b = grad_after.astype(jnp.bfloat16)
    grad_xw = jnp.einsum(
        "scjn,schnp->scjhp", bm_blk, grad_after_b, preferred_element_type=jnp.float32
    )
    grad_bm = grad_bm + jnp.einsum(
        "scjhp,schnp->scjn", xw_val, grad_after_b, preferred_element_type=jnp.float32
    )
    grad_xa = grad_xa + grad_xw * w_end[..., None]
    grad_wend = jnp.sum(grad_xw * xa_f, axis=-1)
    grad_cum_q = grad_cum_q - grad_wend * w_end
    grad_lam = grad_lam + jnp.sum(grad_wend * w_end, axis=2)
    grad_dt_q = jnp.swapaxes(grad_dt_t, 2, 3) + grad_wend * jnp.exp(
        block_log[:, :, None, :] - cum_q
    )
    grad_log = reverse_cumsum(grad_cum_q, 2) + grad_lam[:, :, None, :]
    grad_dt_q = grad_dt_q + grad_log * rate_neg
    grad_alog = jnp.sum(grad_log * log_q, axis=(0, 1, 2))
    grad_raw = grad_dt_q.reshape(row_count, heads_dev) * jax.nn.sigmoid(dt_pre)
    grad_dtb = jnp.sum(grad_raw, axis=0)
    bc_part = jnp.concatenate([grad_bm, grad_cm], axis=-1).reshape(row_count, 2 * state_dim)
    bc_sum = lax.psum(bc_part, "tensor")
    grad_act = jnp.concatenate(
        [
            grad_xa.reshape(seq_count, local_len, inner_dev),
            bc_sum.reshape(seq_count, local_len, 2 * state_dim),
        ],
        axis=-1,
    )
    grad_conv = grad_act * silu_grad(conv_out, sig_conv)
    next_rows = shifted(grad_conv[:, : tap_count - 1], "context", -1)
    extended = jnp.concatenate([grad_conv, next_rows], axis=1)
    grad_pre = conv_all[0] * extended[:, tap_count - 1 : tap_count - 1 + local_len]
    for tap_idx in range(1, tap_count):
        start_at = tap_count - 1 - tap_idx
        grad_pre = grad_pre + conv_all[tap_idx] * extended[:, start_at : start_at + local_len]
    taps_grad = [
        jnp.sum(grad_conv * padded[:, tap_idx : tap_idx + local_len], axis=(0, 1))
        for tap_idx in range(tap_count)
    ]
    grad_taps = jnp.stack(taps_grad + [jnp.sum(grad_conv, axis=(0, 1))], axis=0)
    grad_pre_rows = grad_pre.reshape(row_count, channels)
    grad_zx = jnp.concatenate(
        [grad_gate, grad_pre_rows[:, :inner_dev].astype(jnp.bfloat16)], axis=-1
    )
    grad_bc = grad_pre_rows[:, inner_dev:].astype(jnp.bfloat16)
    grad_raw_b = grad_raw.astype(jnp.bfloat16)
    grad_wzx = contract_rows(normed, grad_zx).reshape(model_dim, 2, inner_dev)
    grad_wbc = contract_rows(normed, grad_bc)
    grad_wdt = contract_rows(normed, grad_raw_b)
    part_in = contract_cols(grad_zx, zx_mat) + contract_cols(grad_raw_b, dt_full)
    grad_normed = lax.psum(part_in, "tensor") + contract_cols(grad_bc, bc_full)
    grad_ng = jnp.sum(grad_normed * stream_in * scale_in, axis=0)
    grad_un = grad_normed * norm_gain
    grad_input = (
        grad_stream
        + scale_in * grad_un
        - stream_in * scale_in**3 * jnp.mean(grad_un * stream_in, axis=-1, keepdims=True)
    )
    summed = lax.psum(
        (
            grad_ng,
            grad_taps[:, :inner_dev],
            grad_taps[:, inner_dev:],
            grad_dtb,
            grad_alog,
            grad_skip,
            grad_og,
            jnp.stack([stream_sq, mixed_sq]),
        ),
        ("shard", "context"),
    )
    zx_share, bc_share, dt_share = (
        lax.psum_scatter(grad_wzx, ("shard", "context"), scatter_dimension=0, tiled=True),
        lax.psum_scatter(grad_wbc, ("shard", "context"), scatter_dimension=0, tiled=True),
        lax.psum_scatter(grad_wdt, ("shard", "context"), scatter_dimension=0, tiled=True),
    )
    entry_count = row_count * model_dim * lax.axis_size("shard") * lax.axis_size("context")
    square_totals = summed[7]
    return (
        stream.astype(jnp.bfloat16).reshape(hidden_in.shape),
        grad_input.reshape(hidden_in.shape),
        summed[0],
        zx_share,
        bc_share,
        dt_share,
        summed[1],
        summed[2],
        summed[3],
        summed[4],
        summed[5],
        summed[6],
        wout_share,
        jnp.sqrt(square_totals[0] / entry_count),
        jnp.sqrt(square_totals[1] / entry_count),
    )


def solution(mesh):
    placed = (
        P("shard", "context", None),
        P(),
        P("shard", None, "tensor"),
        P("shard", None),
        P("shard", "tensor"),
        P(None, "tensor"),
        P(),
        P("tensor"),
        P("tensor"),
        P("tensor"),
        P("tensor"),
        P("tensor", "shard"),
        P("shard", "context", None),
    )
    return jax.shard_map(
        on_device,
        mesh=mesh,
        in_specs=placed,
        out_specs=(
            P("shard", "context", None),
            P("shard", "context", None),
            P(),
            P(("shard", "context"), None, "tensor"),
            P(("shard", "context"), None),
            P(("shard", "context"), "tensor"),
            P(None, "tensor"),
            P(),
            P("tensor"),
            P("tensor"),
            P("tensor"),
            P("tensor"),
            P("tensor", ("shard", "context")),
            P(),
            P(),
        ),
        check_vma=False,
    )
```

profile of v0, /device:TPU:0, one launch (start us, length us, event | category | flops | bytes accessed | tf_op | source)
XLA Modules:
  0.0 1050.1 jit_solution(12844477060453908155)
XLA Ops:
  12.1 15.0 %all_gather.34 = bf16[1536,12]{0,1:T(8,128)(2,1)S(1)} all-gather(bf16[384,12]{0,1:T(8,128)(2,1)S(1)} %copy-done.75), channel_id=1, replica_groups=mesh['shard'=4,'context'=2,'tensor'=4] {'shard'}, dimensions={0}, use_global_device_ids=true | all-gather | bytes 46080 | tf_op jit(solution)/shard_map/all_gather | solution.py:98
  32.2 29.5 %all_gather.33 = bf16[1536,256]{1,0:T(8,128)(2,1)S(1)} all-gather(bf16[384,256]{1,0:T(8,128)(2,1)} %param.24), channel_id=1, replica_groups=mesh['shard'=4,'context'=2,'tensor'=4] {'shard'}, dimensions={0}, use_global_device_ids=true | all-gather | bytes 983040 | tf_op jit(solution)/shard_map/all_gather | solution.py:97
  68.2 46.2 %all-gather.6.cloned.1.call-done = bf16[1536,2,768]{2,1,0:T(2,128)(2,1)} async-done(((bf16[384,2,768]{2,1,0:T(2,128)(2,1)}), bf16[1536,2,768]{2,1,0:T(2,128)(2,1)}) %all-gather.6.cloned.1.call-update) | async-done | bytes 4718608 | tf_op jit(solution)/shard_map/all_gather | solution.py:96
  117.8 5.1 fusion.61
  140.0 5.4 all-reduce
  151.0 10.0 multiply_convert_fusion.3
  167.4 3.9 reshape.673
  176.4 12.2 %while.60 = (s32[]{:T(128)}, f32[1,12,128,64]{3,2,1,0:T(8,128)S(1)}, f32[4,1,12,128,64]{4,3,2,1,0:T(8,128)}, f32[4,1,12]{2,1,0:T(1,128)}, f32[4,1,12,128,64]{3,4,2,0,1:T(8,128)}, /*index=5*/s32[]{:T(128)}, s32[]{:T(128)}) while((s32[]{:T(128)}, f32[1,12,128,64]{3,2,1,0:T(8,128)S(1)}, f32[4,1,12,128,64]{4,3,2,1,0:T(8,128)}, ...), condition=%wide.region_4.5_spmd.clone, body=%wide.region_3.4_spmd.clone.sunk | while | flops 393219 | bytes 3932912 | solution.py:156
  192.9 3.6 copy.426
  196.5 5.2 reshape.700
  201.7 10.5 %all-gather.1 = f32[2,12,128,64]{2,3,1,0:T(8,128)} all-gather(f32[1,12,128,64]{2,3,1,0:T(8,128)S(1)} %copy.421), channel_id=3, replica_groups=mesh['shard'=4,'context'=2,'tensor'=4] {'context'}, dimensions={0}, use_global_device_ids=true | all-gather | bytes 1179648 | tf_op jit(solution)/shard_map/all_gather | solution.py:21
  212.2 6.7 fusion.32
  218.9 4.3 while.61
  223.2 6.2 bitcast_add_fusion.5
  233.9 3.6 copy.429
  237.5 5.4 multiply_reduce_fusion.10
  242.9 5.6 psum.91
  248.5 8.6 multiply_reduce_fusion.8
  257.1 6.7 psum.93
  263.9 8.0 fusion.52
  277.7 3.9 reshape.688
  281.5 4.4 fusion.73
  288.0 12.2 %while.62 = (s32[]{:T(128)}, f32[1,12,128,64]{3,2,1,0:T(8,128)S(1)}, f32[4,1,12,128,64]{4,3,2,1,0:T(8,128)}, f32[4,1,12,128,64]{3,4,2,0,1:T(8,128)}, f32[4,1,12]...) while((s32[]{:T(128)}, f32[1,12,128,64]{3,2,1,0:T(8,128)S(1)}, ...), condition=%wide.region_15.16_spmd.clone, body=%wide.region_14.15_spmd.clone.sunk | while | flops 393220 | bytes 3932424 | solution.py:223
  300.5 10.7 %all-gather.2 = f32[2,12,128,64]{2,3,1,0:T(8,128)S(1)} all-gather(f32[1,12,128,64]{2,3,1,0:T(8,128)S(1)} %copy.438), channel_id=4, replica_groups=mesh['shard'=4,'context'=2,'tensor'=4] {'context'}, dimensions={0}, use_global_device_ids=true | all-gather | bytes 1179648 | tf_op jit(solution)/shard_map/all_gather | solution.py:21
  313.5 3.5 fusion.55
  318.9 4.0 fusion.77
  323.0 11.9 %fusion.12 = (f32[4,12,256]{2,1,0:T(8,128)}, f32[4,12,256]{2,1,0:T(8,128)}, f32[4,12,256]{2,1,0:T(8,128)}, f32[4,256,256]{2,1,0:T(8,128)}) fusion(f32[4,12,256]{2,1,0:T(8,128)S(1)} %copy-done.61, f32[256,256]{1,0:T(8,128)S(1)} %copy-done.46, f32[4,12,256]{2,1,0:T(8,128)S(1)} %copy-done.59, f32[4,256,256]{2,1,0:T(8,128)S(1)} %copy-done.33, ...), kind=kOutput, calls=%fused_computation.32 | convolution fusion | flops 446394368 | bytes 5816320 | tf_op jit(solution)/shard_map/scihp,scjhp->schij/dot_general | solution.py:200
  335.1 3.9 fusion.54
  349.4 5.1 reduce-window.16
  360.4 7.3 fusion.51
  372.8 3.7 copy.451
  390.7 25.7 %all-reduce.6.cloned.1.call-done = f32[1,1024,256]{2,1,0:T(8,128)} async-done(((f32[1,1024,256]{2,1,0:T(8,128)}), f32[1,1024,256]{2,1,0:T(8,128)}) %all-reduce.6.cloned.1.call-update) | async-done | bytes 1048592 | tf_op jit(solution)/shard_map/psum | solution.py:260
  416.4 11.7 %fusion.119 = (f32[1024]{0:T(1024)S(1)}, f32[1024]{0:T(1024)S(1)}, f32[1024]{0:T(1024)S(1)}, f32[1024]{0:T(1024)S(1)}, f32[1024]{0:T(1024)S(1)}, /*index=5*/f32[1,1024,1024]{2,1,0:T(8,128)S(1)}) fusion(f32[1024,256]{1,0:T(8,128)} %fusion.129, f32[1024,768]{1,0:T(8,128)} %copy-done.9, f32[1,1024,1024]{2,1,0:T(8,128)} %copy-done.7, ...), kind=kLoop, calls=%fused_computation.207 | loop fusion | flops 23063552 | bytes 21004288 | tf_op jit(solution)/shard_map/reduce_sum | solution.py:279
  429.7 5.1 fusion.118
  440.4 5.1 fusion.70
  445.5 3.7 convolution_add_fusion.1
  449.3 3.8 fusion.69
  453.1 4.7 copy.481
  457.8 10.5 fusion.49
  471.8 7.7 fusion.56
  484.9 221.3 %all-reduce.8.cloned.1.call-done = (f32[1024,1536]{1,0:T(8,128)}, f32[1024,1536]{1,0:T(8,128)}) async-done(((f32[1024,1536]{1,0:T(8,128)}, f32[1024,1536]{1,0:T(8,128)}), (f32[1024,1536]{1,0:T(8,128)}, f32[1024,1536]{1,0:T(8,128)})) %all-reduce.8.cloned.1.call-update) | async-done | bytes 12582928 | tf_op jit(solution)/shard_map/psum | solution.py:183
  706.1 4.3 convolution_add_fusion
  713.4 5.9 multiply_reduce_fusion.3
  720.7 41.1 %all-reduce.1 = (f32[1536]{0:T(1024)}, f32[5,768]{1,0:T(8,128)}, f32[5,256]{1,0:T(8,128)}, f32[12]{0:T(128)}, f32[12]{0:T(128)}, /*index=5*/f32[12]{0:T(128)}, f32[768]{0:T(1024)}, f32[2]{0:T(128)S(1)}) all-reduce(f32[1536]{0:T(1024)S(1)} %get-tuple-element.717, ...), channel_id=1, replica_groups=mesh['shard'=4,'context'=2,'tensor'=4] {'shard','context'}, use_global_device_ids=true, to_apply=%region_34.35 | all-reduce | flops 7462 | bytes 59696 | tf_op jit(solution)/shard_map/psum | solution.py:298
  763.8 6.4 fusion.19
  770.2 103.1 %reduce-scatter.7.cloned.1.call-done = f32[192,2,768]{2,0,1:T(8,128)} async-done(((f32[1536,2,768]{2,0,1:T(8,128)}), f32[192,2,768]{2,0,1:T(8,128)}) %reduce-scatter.7.cloned.1.call-update) | async-done | bytes 1179664 | tf_op jit(solution)/shard_map/reduce_scatter | solution.py:312
  876.4 65.6 %reduce-scatter.9.cloned.1.call-done = f32[192,256]{1,0:T(8,128)} async-done(((f32[1536,256]{1,0:T(8,128)}), f32[192,256]{1,0:T(8,128)}) %reduce-scatter.9.cloned.1.call-update) | async-done | bytes 196624 | tf_op jit(solution)/shard_map/reduce_scatter | solution.py:313
  942.1 98.7 %reduce-scatter.11.cloned.1.call-done = f32[768,192]{0,1:T(8,128)} async-done(((f32[768,1536]{0,1:T(8,128)}), f32[768,192]{0,1:T(8,128)}) %reduce-scatter.11.cloned.1.call-update) | async-done | bytes 589840 | tf_op jit(solution)/shard_map/reduce_scatter | solution.py:190
  (376 shorter events, 164.3 us)
Async XLA Ops:
  7.2 19.9 %copy-start.85 = (f32[12]{0:T(128)S(1)}, f32[12]{0:T(128)}, u32[]{:S(2)}) copy-start(f32[12]{0:T(128)} %param.29) | copy-start | bytes 148
  7.2 19.9 %copy-start.50 = (f32[1536]{0:T(1024)S(1)}, f32[1536]{0:T(1024)}, u32[]{:S(2)}) copy-start(f32[1536]{0:T(1024)} %param.22) | copy-start | bytes 18436
  7.2 107.2 %all-gather.6.cloned.1.call-start = ((), (), s32[]{:S(2)}) async-start(), calls=%async_computation.4 | async-start | bytes 5898240 | tf_op jit(solution)/shard_map/all_gather | solution.py:96
  7.9 240.6 %all-gather.8.cloned.1.call-start = ((), (), s32[]{:S(2)}) async-start(), calls=%async_computation.5 | async-start | bytes 2949120 | tf_op jit(solution)/shard_map/all_gather | solution.py:99
  8.7 407.7 %all-reduce.6.cloned.1.call-start = ((), (), s32[]{:S(2)}) async-start(), calls=%async_computation.6 | async-start | bytes 2097152 | tf_op jit(solution)/shard_map/psum | solution.py:260
  8.7 18.4 %copy-start.3 = (bf16[1,1024,1536]{2,1,0:T(8,128)(2,1)S(1)}, bf16[1,1024,1536]{2,1,0:T(8,128)(2,1)}, u32[]{:S(2)}) copy-start(bf16[1,1024,1536]{2,1,0:T(8,128)(2,1)} %param.21) | copy-start | bytes 9437188
  12.1 105.7 %copy-start.62 = (f32[1024]{0:T(1024)}, f32[1024]{0:T(1024)S(1)}, u32[]{:S(2)}) copy-start(f32[1024]{0:T(1024)S(1)} %get-tuple-element.803) | copy-start | bytes 12292
  28.0 33.7 %copy-start.1 = (bf16[1024,1536]{1,0:T(8,128)(2,1)}, bf16[1024,1536]{1,0:T(8,128)(2,1)S(1)}, u32[]{:S(2)}) copy-start(bf16[1024,1536]{1,0:T(8,128)(2,1)S(1)} %fusion.16) | copy-start | bytes 9437188
  29.7 34.0 %copy-start.40 = (f32[1,4,256,12]{2,1,3,0:T(4,128)}, f32[1,4,256,12]{2,1,3,0:T(4,128)S(1)}, u32[]{:S(2)}) copy-start(f32[1,4,256,12]{2,1,3,0:T(4,128)S(1)} %reshape.676) | copy-start | bytes 147460
  65.4 52.4 %copy-start.31 = (f32[1,4,256,12]{2,1,3,0:T(4,128)}, f32[1,4,256,12]{2,1,3,0:T(4,128)S(1)}, u32[]{:S(2)}) copy-start(f32[1,4,256,12]{2,1,3,0:T(4,128)S(1)} %get-tuple-element.778) | copy-start | bytes 147460
  66.8 82.1 %copy-start.34 = (f32[1,4,256,12]{2,1,3,0:T(4,128)}, f32[1,4,256,12]{2,1,3,0:T(4,128)S(1)}, u32[]{:S(2)}) copy-start(f32[1,4,256,12]{2,1,3,0:T(4,128)S(1)} %reshape.682) | copy-start | bytes 147460
  129.0 22.0 %collective-permute-start = (f32[1,3,1024]{2,1,0:T(4,128)}, f32[1,3,1024]{2,1,0:T(4,128)S(1)}, u32[]{:S(2)}, u32[]{:S(2)}) collective-permute-start(f32[1,3,1024]{2,1,0:T(4,128)} %slice.128), channel_id=1, source_target_pairs={{0,4},{1,5},{2,6},{3,7},{8,12},{9,13},{10,14},{11,15},{16,20},{17,... | collective-permute-start | bytes 36872 | tf_op jit(solution)/shard_map/ppermute | solution.py:16
  151.0 10.0 copy-start.64
  196.5 15.7 %copy-start.45 = (f32[256,256]{1,0:T(8,128)S(1)}, f32[256,256]{1,0:T(8,128)}, u32[]{:S(2)}) copy-start(f32[256,256]{1,0:T(8,128)} %get-tuple-element.813) | copy-start | bytes 786436
  196.5 15.7 %copy-start.52 = (pred[256,256]{1,0:T(8,128)(4,1)S(1)}, pred[256,256]{1,0:T(8,128)(4,1)}, u32[]{:S(2)}) copy-start(pred[256,256]{1,0:T(8,128)(4,1)} %get-tuple-element.812) | copy-start | bytes 196612
  196.5 15.7 %copy-start.58 = (f32[4,12,256]{2,1,0:T(8,128)S(1)}, f32[4,12,256]{2,1,0:T(8,128)}, u32[]{:S(2)}) copy-start(f32[4,12,256]{2,1,0:T(8,128)} %copy.408) | copy-start | bytes 147460
  196.5 15.7 %copy-start.60 = (f32[4,12,256]{2,1,0:T(8,128)S(1)}, f32[4,12,256]{2,1,0:T(8,128)}, u32[]{:S(2)}) copy-start(f32[4,12,256]{2,1,0:T(8,128)} %copy.410) | copy-start | bytes 147460
  237.5 11.1 %copy-start.80 = (f32[768]{0:T(1024)S(1)}, f32[768]{0:T(1024)}, u32[]{:S(2)}) copy-start(f32[768]{0:T(1024)} %param.31) | copy-start | bytes 9220
  248.5 15.4 %copy-start.72 = (f32[1024]{0:T(1024)}, f32[1024]{0:T(1024)S(1)}, u32[]{:S(2)}) copy-start(f32[1024]{0:T(1024)S(1)} %get-tuple-element.805) | copy-start | bytes 12292
  323.0 11.9 %copy-start.17 = (bf16[1,1024,128]{2,1,0:T(8,128)(2,1)S(1)}, bf16[1,1024,128]{2,1,0:T(8,128)(2,1)}, u32[]{:S(2)}) copy-start(bf16[1,1024,128]{2,1,0:T(8,128)(2,1)} %get-tuple-element.788) | copy-start | bytes 786436
  323.0 12.0 %copy-start.69 = (f32[4,12]{1,0:T(4,128)S(1)}, f32[4,12]{1,0:T(4,128)}, u32[]{:S(2)}) copy-start(f32[4,12]{1,0:T(4,128)} %get-tuple-element.806) | copy-start | bytes 580
  323.0 12.0 %copy-start.70 = (f32[4,12]{1,0:T(4,128)S(1)}, f32[4,12]{1,0:T(4,128)}, u32[]{:S(2)}) copy-start(f32[4,12]{1,0:T(4,128)} %get-tuple-element.807) | copy-start | bytes 580
  343.3 14.2 %copy-start.12 = (f32[1024,768]{0,1:T(8,128)S(1)}, f32[1024,768]{0,1:T(8,128)}, u32[]{:S(2)}) copy-start(f32[1024,768]{0,1:T(8,128)} %copy.433) | copy-start | bytes 9437188
  378.6 7.7 copy-start.48
  378.6 8.7 copy-start.41
  378.6 8.7 copy-start.78
  378.6 9.9 copy-start.42
  378.6 10.0 copy-start.2
  381.9 101.3 %reduce-scatter.13.cloned.1.call-start = ((), (), s32[]{:S(2)}) async-start(), calls=%async_computation.10 | async-start | bytes 884736
  388.7 27.8 %copy-start.65 = (f32[1,3,1024]{2,1,0:T(4,128)S(1)}, f32[1,3,1024]{2,1,0:T(4,128)}, u32[]{:S(2)}) copy-start(f32[1,3,1024]{2,1,0:T(4,128)} %copy-done.64) | copy-start | bytes 36868
  390.6 315.5 %all-reduce.8.cloned.1.call-start = ((), (), s32[]{:S(2)}) async-start(), calls=%async_computation.11 | async-start | bytes 25165824 | tf_op jit(solution)/shard_map/psum | solution.py:183
  416.4 13.3 %copy-start.14 = (f32[1024,768]{1,0:T(8,128)S(1)}, f32[1024,768]{1,0:T(8,128)}, u32[]{:S(2)}) copy-start(f32[1024,768]{1,0:T(8,128)} %get-tuple-element.776) | copy-start | bytes 9437188
  416.4 13.3 %copy-start.73 = (f32[1024]{0:T(1024)S(1)}, f32[1024]{0:T(1024)}, u32[]{:S(2)}) copy-start(f32[1024]{0:T(1024)} %copy-done.72) | copy-start | bytes 12292
  416.4 13.3 %copy-start.81 = (f32[768]{0:T(1024)S(1)}, f32[768]{0:T(1024)}, u32[]{:S(2)}) copy-start(f32[768]{0:T(1024)} %param.31) | copy-start | bytes 9220
  416.4 13.3 %copy-start.84 = (bf16[768,1536]{1,0:T(8,128)(2,1)S(1)}, bf16[768,1536]{1,0:T(8,128)(2,1)}, u32[]{:S(2)}) copy-start(bf16[768,1536]{1,0:T(8,128)(2,1)} %all-gather.8.cloned.1.call-done) | copy-start | bytes 7077892
  416.4 22.2 %slice-start = ((s8[4718592]{0:T(1024)(128)(4,1)}), s8[4194304]{0:T(1024)(128)(4,1)S(1)}, s32[]{:S(2)}) async-start(s8[4718592]{0:T(1024)(128)(4,1)} %bitcast.347), calls=%async_computation.12 | async-start | bytes 8388608
  428.2 10.4 slice-start.1
  428.2 6.6 collective-permute-start.1
  449.2 424.0 %reduce-scatter.7.cloned.1.call-start = ((), (), s32[]{:S(2)}) async-start(), calls=%async_computation.7 | async-start | bytes 10616832 | tf_op jit(solution)/shard_map/reduce_scatter | solution.py:312
  468.3 473.8 %reduce-scatter.9.cloned.1.call-start = ((), (), s32[]{:S(2)}) async-start(), calls=%async_computation.8 | async-start | bytes 1769472 | tf_op jit(solution)/shard_map/reduce_scatter | solution.py:313
  471.5 569.3 %reduce-scatter.11.cloned.1.call-start = ((), (), s32[]{:S(2)}) async-start(), calls=%async_computation.9 | async-start | bytes 5308416 | tf_op jit(solution)/shard_map/reduce_scatter | solution.py:190
  484.8 225.6 %copy-start.49 = (f32[5,1024]{1,0:T(8,128)}, f32[5,1024]{1,0:T(8,128)S(1)}, u32[]{:S(2)}) copy-start(f32[5,1024]{1,0:T(8,128)S(1)} %stack.32) | copy-start | bytes 61444
  706.1 7.3 copy-start.18
  710.5 8.8 copy-start
  713.4 7.3 slice-start.2
  713.4 7.3 slice-start.3
  713.4 7.3 copy-start.79
  713.4 50.4 %copy-start.71 = (f32[1024]{0:T(1024)S(1)}, f32[1024]{0:T(1024)}, u32[]{:S(2)}) copy-start(f32[1024]{0:T(1024)} %get-tuple-element.802) | copy-start | bytes 12292
  (52 other events, 192.2 us)
Sparse Core Ops, SparseCore 0:
  9.6 104.7 all-gather.5
  116.0 48.6 all-gather.7
  382.0 34.3 all-reduce.5
  419.6 63.6 reduce-scatter.12
  486.2 219.8 all-reduce.7
  709.6 163.6 reduce-scatter.6
  877.2 64.8 reduce-scatter.8
  946.3 94.4 reduce-scatter.10
where the time goes:
time: 1060 us; the launch traced here: 1050 us
  waiting for transfers between devices  565 us (53%)
  local copies, waits for them, and re-layouts  125 us (12%)
  blocking collectives  125 us (12%)
  matrix products  111 us (10%)
  other arithmetic  99.2 us (9%)
  between operations  19.7 us (2%)
    psum x1, waiting for transfers between devices, on_device(): lax.psum(jnp.dot(out_in, out_full, preferred_element_type=jnp.float32), '...  221 us
    reduce_scatter x1, waiting for transfers between devices, on_device(): lax.psum_scatter(grad_wzx, ('shard', 'context'), scatter_dimension=0, til...  103 us
    reduce_scatter x1, waiting for transfers between devices, on_device(): lax.psum_scatter(grad_wout, ('shard', 'context'), scatter_dimension=1, ti...  98.7 us
    reduce_scatter x1, waiting for transfers between devices, on_device(): lax.psum_scatter(grad_wbc, ('shard', 'context'), scatter_dimension=0, til...  65.6 us
    all_gather x1, waiting for transfers between devices, on_device(): lax.all_gather(w_in_zx, 'shard', axis=0, tiled=True)  46.2 us
    psum x1, blocking collectives, on_device(): lax.psum((grad_ng, grad_taps[:, :inner_dev], grad_taps[:, inner_dev:], gr...  41.1 us
    all_gather x1, blocking collectives, on_device(): lax.all_gather(w_in_bc, 'shard', axis=0, tiled=True)  29.5 us
    psum x1, waiting for transfers between devices, on_device(): bc_sum = lax.psum(bc_part, 'tensor')  25.7 us
  transfers between devices with their start and end apart: 10, of which 7 were waited for; matrix products, arithmetic and copies ran while one was open for 20% of the time, Pallas kernels for 0%

commit v1 on v0

v1 whole, which is shorter than its diff:
```python
import functools

import jax
import jax.numpy as jnp
from jax import lax
from jax.experimental import pallas as pl
from jax.experimental.pallas import tpu as pltpu
from jax.sharding import PartitionSpec as P

CH = 256
EPSILON = 1e-05
LANES = 128
HALO = 8
F32 = jnp.float32
BF16 = jnp.bfloat16


def swap_pairs(size, by):
    return [(i, i ^ by) for i in range(size)]


def butterfly(value, axis):
    size = lax.axis_size(axis)
    if size & (size - 1):
        return lax.psum(value, axis)
    by = 1
    while by < size:
        value = value + lax.ppermute(value, axis, swap_pairs(size, by))
        by *= 2
    return value


def shifted(array, axis, by):
    length = lax.axis_size(axis)
    pairs = [(i, i + by) for i in range(length) if 0 <= i + by < length]
    return lax.ppermute(array, axis, pairs)


def joint_pairs(size, context, sources, move):
    return [(i * context + c, move(i, c)[0] * context + move(i, c)[1]) for i in sources for c in range(context)]


def gather_weights(local):
    shards, parts = lax.axis_size("shard"), lax.axis_size("context")
    here, side = lax.axis_index("shard"), lax.axis_index("context")
    rows = local.shape[0] // parts
    own = lax.dynamic_slice_in_dim(local, side * rows, rows, 0)
    axes = ("shard", "context")
    if parts != 2 or shards > 8:
        return lax.all_gather(own, axes, axis=0, tiled=True)
    whole_rows = shards * parts * rows
    full = jnp.zeros((whole_rows + rows, local.shape[1]), local.dtype)
    full = lax.dynamic_update_slice_in_dim(full, local, here * parts * rows, 0)

    def put(full, piece, valid, source, part):
        at = jnp.where(valid, (source * parts + part) * rows, whole_rows)
        return lax.dynamic_update_slice_in_dim(full, piece, at, 0)

    plus = minus = own
    for k in range(1, shards):
        plus = lax.ppermute(plus, axes, joint_pairs(shards, parts, range(k - 1, shards - 1), lambda i, c: (i + 1, c)))
        minus = lax.ppermute(minus, axes, joint_pairs(shards, parts, range(1, shards - k + 1), lambda i, c: (i - 1, c)))
        across_plus = lax.ppermute(plus, axes, joint_pairs(shards, parts, range(k, shards), lambda i, c: (i, 1 - c)))
        across_minus = lax.ppermute(minus, axes, joint_pairs(shards, parts, range(0, shards - k), lambda i, c: (i, 1 - c)))
        full = put(full, plus, here >= k, here - k, side)
        full = put(full, minus, here + k < shards, here + k, side)
        full = put(full, across_plus, here >= k, here - k, 1 - side)
        full = put(full, across_minus, here + k < shards, here + k, 1 - side)
    return full


def scatter_grad(keep, send):
    shards = lax.axis_size("shard")
    here = lax.axis_index("shard")
    got = lax.ppermute(send, "context", swap_pairs(2, 1))
    summed = (keep.astype(F32) + got.astype(F32)).astype(BF16)
    piece = lambda at: lax.dynamic_index_in_dim(summed, jnp.clip(at, 0, shards - 1), 0, False)
    plus = minus = None
    for k in range(1, shards):
        up, down = piece(here + shards - k), piece(here - shards + k)
        if plus is not None:
            up = (up.astype(F32) + plus.astype(F32)).astype(BF16)
            down = (down.astype(F32) + minus.astype(F32)).astype(BF16)
        plus = lax.ppermute(up, "shard", [(i, i + 1) for i in range(k)])
        minus = lax.ppermute(down, "shard", [(shards - 1 - i, shards - 2 - i) for i in range(k)])
    return piece(here).astype(F32) + plus.astype(F32) + minus.astype(F32)


def tensor_pairs(size, bit):
    return swap_pairs(size, bit)


def reduce_mine(keep, send, size):
    got = lax.ppermute(send, "tensor", swap_pairs(size, 1))
    rows = keep.shape[0] // 2
    other = (keep[rows:].astype(F32) + got[rows:].astype(F32)).astype(BF16)
    got_mine = lax.ppermute(other, "tensor", swap_pairs(size, 2))
    return keep[:rows].astype(F32) + got[:rows].astype(F32) + got_mine.astype(F32)


def assemble_kernel(place, own, chip, core_a, core_b, out):
    r = pl.program_id(0)
    for k, ref in enumerate((own, chip, core_a, core_b)):

        @pl.when(r == k)
        def _():
            out[...] = ref[...].astype(out.dtype)


def gather_quarters(mine, place, size, dtype):
    chip = lax.ppermute(mine, "tensor", swap_pairs(size, 2))
    core_a = lax.ppermute(mine, "tensor", swap_pairs(size, 1))
    core_b = lax.ppermute(chip, "tensor", swap_pairs(size, 1))
    rows, cols = mine.shape
    piece = pl.BlockSpec((rows, cols), lambda r, q: (0, 0))
    return pl.pallas_call(
        assemble_kernel,
        name="assemble",
        grid_spec=pltpu.PrefetchScalarGridSpec(
            num_scalar_prefetch=1,
            grid=(4,),
            in_specs=[piece] * 4,
            out_specs=pl.BlockSpec((rows, cols), lambda r, q: (r ^ q[0], 0)),
        ),
        out_shape=jax.ShapeDtypeStruct((4 * rows, cols), dtype),
        compiler_params=params(),
        cost_estimate=cost(0, 12 * rows * cols + 0, 0),
    )(place, mine, chip, core_a, core_b)


def dot_nn(a, b):
    return lax.dot_general(a, b, (((1,), (0,)), ((), ())), preferred_element_type=F32)


def dot_nt(a, b):
    return lax.dot_general(a, b, (((1,), (1,)), ((), ())), preferred_element_type=F32)


def dot_tn(a, b):
    return lax.dot_general(a, b, (((0,), (0,)), ((), ())), preferred_element_type=F32)


def by_heads(values, onehot):
    high = values.astype(BF16)
    low = (values - high.astype(F32)).astype(BF16)
    return dot_nn(high, onehot) + dot_nn(low, onehot)


def by_heads_t(values, onehot):
    high = values.astype(BF16)
    low = (values - high.astype(F32)).astype(BF16)
    return dot_nt(high, onehot) + dot_nt(low, onehot)


def row_of(values, onehot):
    return by_heads(jnp.broadcast_to(values, (8, values.shape[1])), onehot)[0:1]


def fold_rows(values):
    rows, cols = values.shape
    return jnp.sum(values.reshape(rows // 8, 8, cols), axis=0)


def exact_parts(values):
    high = values.astype(BF16)
    rest = values - high.astype(F32)
    mid = rest.astype(BF16)
    low = (rest - mid.astype(F32)).astype(BF16)
    return high, mid, low


def sigmoid(values):
    return 1.0 / (1.0 + jnp.exp(-values))


def whole(shape):
    zeros = (0,) * len(shape)
    return pl.BlockSpec(shape, lambda *_: zeros)


def params(semantics=("arbitrary",)):
    return pltpu.CompilerParams(dimension_semantics=semantics, vmem_limit_bytes=60 * 1024 * 1024)


def cost(flops, nbytes, exps=0):
    return pl.CostEstimate(flops=int(flops), bytes_accessed=int(nbytes), transcendentals=int(exps))


def conv_kernel(normed, halo, weight, taps, act, pre):
    rows = normed.shape[0]
    tap_count = 4
    w = weight[...]
    pre[0:HALO, :] = dot_nn(halo[...], w)
    pre[HALO:, :] = dot_nn(normed[...], w)
    first = HALO - tap_count + 1
    out = taps[tap_count : tap_count + 1, :] + taps[0:1, :] * pre[first : first + rows, :]
    for k in range(1, tap_count):
        out = out + taps[k : k + 1, :] * pre[first + k : first + k + rows, :]
    act[...] = (out * sigmoid(out)).astype(BF16)


def conv_front(normed, halo, weight, taps):
    rows, dim = normed.shape
    cols = taps.shape[1]
    tile = 256
    return pl.pallas_call(
        conv_kernel,
        name="conv_front",
        grid=(cols // tile,),
        in_specs=[
            whole((rows, dim)),
            whole((HALO, dim)),
            pl.BlockSpec((dim, tile), lambda j: (0, j)),
            pl.BlockSpec((8, tile), lambda j: (0, j)),
        ],
        out_specs=[
            pl.BlockSpec((rows, tile), lambda j: (0, j)),
            pl.BlockSpec((rows + HALO, tile), lambda j: (0, j)),
        ],
        out_shape=[
            jax.ShapeDtypeStruct((rows, cols), BF16),
            jax.ShapeDtypeStruct((rows + HALO, cols), F32),
        ],
        compiler_params=params(),
        cost_estimate=cost(2 * rows * dim * cols, 2 * (rows + cols) * dim + 6 * rows * cols, rows * cols),
    )(normed, halo, weight, taps)


def step_kernel(normed, weight, bias, rate, dt, sig, cum, seq, cum_t, before):
    @pl.when(pl.program_id(0) == 0)
    def _():
        before[...] = jnp.zeros_like(before)

    raw = dot_nn(normed[...], weight[...]) + bias[...]
    small = jnp.exp(-jnp.abs(raw))
    dt_val = jnp.maximum(raw, 0.0) + jnp.log1p(small)
    dt[...] = dt_val
    sig[...] = sigmoid(raw)
    rows = raw.shape[0]
    lower = (
        lax.broadcasted_iota(jnp.int32, (rows, rows), 0) >= lax.broadcasted_iota(jnp.int32, (rows, rows), 1)
    ).astype(BF16)
    total = jnp.zeros_like(raw)
    for part in exact_parts(dt_val * rate[...]):
        total = total + dot_nn(lower, part)
    cum[...] = total
    seq[...] = total + before[0:1, :]
    before[...] = before[...] + jnp.broadcast_to(total[rows - 1 : rows, :], before.shape)
    cum_t[...] = jnp.transpose(total)[0:16, :]


def step_sizes(normed, weight, bias, rate, col):
    rows, dim = normed.shape
    block = pl.BlockSpec((CH, LANES), lambda b: (b, 0))
    wide = jax.ShapeDtypeStruct((rows, LANES), F32)
    return pl.pallas_call(
        step_kernel,
        name="step_sizes",
        grid=(rows // CH,),
        in_specs=[
            pl.BlockSpec((CH, dim), lambda b: (b, 0)),
            pl.BlockSpec((dim, LANES), lambda b: (0, col)),
            whole((1, LANES)),
            whole((1, LANES)),
        ],
        out_specs=[block, block, block, block, pl.BlockSpec((16, CH), lambda b: (0, b))],
        out_shape=[wide, wide, wide, wide, jax.ShapeDtypeStruct((16, rows), F32)],
        scratch_shapes=[pltpu.VMEM((8, LANES), F32)],
        compiler_params=params(),
        cost_estimate=cost(2 * rows * dim * LANES, 2 * rows * dim + 20 * rows * LANES, 3 * rows * LANES),
    )(normed, weight, bias, rate)


def ssd_kernel(heads, xa_ref, bm_ref, cm_ref, dt_ref, cum_ref, cum_t_ref, skip, onehot, y_ref, start_ref, end_ref, state):
    @pl.when(pl.program_id(0) == 0)
    def _():
        state[...] = jnp.zeros_like(state)

    hot = onehot[...]
    xa = xa_ref[...].astype(F32)
    bm, cm, cum, cum_t = bm_ref[...], cm_ref[...], cum_ref[...], cum_t_ref[...]
    rows = cum.shape[0]
    last = cum[rows - 1 : rows, :]
    x_dt = xa * by_heads(dt_ref[...], hot)
    before = state[...]
    start_ref[0] = before
    y_ref[...] = by_heads(jnp.exp(cum), hot) * dot_nn(cm, before.astype(BF16)) + skip[...] * xa
    to_end = (x_dt * by_heads(jnp.exp(last - cum), hot)).astype(BF16)
    after = row_of(jnp.exp(last), hot) * before + dot_tn(bm, to_end)
    state[...] = after
    end_ref[...] = after
    x_low = x_dt.astype(BF16)
    scores = dot_nt(cm, bm)
    mask = lax.broadcasted_iota(jnp.int32, (rows, rows), 0) >= lax.broadcasted_iota(jnp.int32, (rows, rows), 1)
    width = xa.shape[1] // heads
    per = LANES // width
    lane = lax.broadcasted_iota(jnp.int32, (rows, LANES), 1) // width
    for group in range(heads // per):
        at = slice(group * LANES, (group + 1) * LANES)
        x_group = x_low[:, at]
        total = y_ref[:, at]
        for k in range(per):
            h = group * per + k
            gap = jnp.where(mask, cum[:, h : h + 1] - cum_t[h : h + 1, :], 0.0)
            weights = jnp.where(mask, jnp.exp(gap) * scores, 0.0).astype(BF16)
            total = total + dot_nn(weights, jnp.where(lane == k, x_group, jnp.zeros_like(x_group)))
        y_ref[:, at] = total


def ssd_forward(act, dt, cum, cum_t, skip, onehot, heads):
    rows = act.shape[0]
    inner = onehot.shape[1]
    blocks = rows // CH
    col = inner // LANES
    wide = pl.BlockSpec((CH, LANES), lambda b: (b, 0))
    return pl.pallas_call(
        functools.partial(ssd_kernel, heads),
        name="ssd_forward",
        grid=(blocks,),
        in_specs=[
            pl.BlockSpec((CH, inner), lambda b: (b, 0)),
            pl.BlockSpec((CH, LANES), lambda b: (b, col)),
            pl.BlockSpec((CH, LANES), lambda b: (b, col + 1)),
            wide,
            wide,
            pl.BlockSpec((16, CH), lambda b: (0, b)),
            whole((1, inner)),
            whole((LANES, inner)),
        ],
        out_specs=[
            pl.BlockSpec((CH, inner), lambda b: (b, 0)),
            pl.BlockSpec((1, LANES, inner), lambda b: (b, 0, 0)),
            whole((LANES, inner)),
        ],
        out_shape=[
            jax.ShapeDtypeStruct((rows, inner), F32),
            jax.ShapeDtypeStruct((blocks, LANES, inner), F32),
            jax.ShapeDtypeStruct((LANES, inner), F32),
        ],
        scratch_shapes=[pltpu.VMEM((LANES, inner), F32)],
        compiler_params=params(),
        cost_estimate=cost(6 * rows * CH * inner, 12 * rows * inner, rows * CH * heads),
    )(act, act, act, dt, cum, cum_t, skip, onehot)


def gate_kernel(normed, grad, w_gate, w_out, y_in, cm, seq, state, gain, onehot, gate_ref, y_ref, gon_ref, stat_ref):
    gate = dot_nn(normed[...], w_gate[...])
    grad_on = dot_nn(grad[...], w_out[...])
    y = y_in[...] + by_heads(jnp.exp(seq[...]), onehot[...]) * dot_nn(cm[...], state[...])
    gated = y * (gate * sigmoid(gate))
    gate_ref[...] = gate
    y_ref[...] = y
    gon_ref[...] = grad_on
    square = jnp.sum(gated * gated, axis=1, keepdims=True)
    inner = jnp.sum(grad_on * gain[...] * gated, axis=1, keepdims=True)
    lane = lax.broadcasted_iota(jnp.int32, (gate.shape[0], LANES), 1)
    both = jnp.where(lane == 0, square, jnp.where(lane == 1, inner, 0.0))
    stat_ref[...] = jnp.transpose(both)[0:8, :]


def gate_stage(normed, grad, w_rest, y_in, act, seq, state, gain, onehot):
    rows, dim = normed.shape
    inner = onehot.shape[1]
    col = inner // LANES
    block = pl.BlockSpec((CH, inner), lambda b: (b, 0))
    full = jax.ShapeDtypeStruct((rows, inner), F32)
    return pl.pallas_call(
        gate_kernel,
        name="gate_stage",
        grid=(rows // CH,),
        in_specs=[
            pl.BlockSpec((CH, dim), lambda b: (b, 0)),
            pl.BlockSpec((CH, dim), lambda b: (b, 0)),
            pl.BlockSpec((dim, inner), lambda b: (0, 0)),
            pl.BlockSpec((dim, inner), lambda b: (0, 1)),
            block,
            pl.BlockSpec((CH, LANES), lambda b: (b, col + 1)),
            pl.BlockSpec((CH, LANES), lambda b: (b, 0)),
            whole((LANES, inner)),
            whole((1, inner)),
            whole((LANES, inner)),
        ],
        out_specs=[block, block, block, pl.BlockSpec((8, CH), lambda b: (0, b))],
        out_shape=[full, full, full, jax.ShapeDtypeStruct((8, rows), F32)],
        compiler_params=params(),
        cost_estimate=cost(4 * rows * dim * inner, 16 * rows * inner + 4 * rows * dim, rows * inner),
    )(normed, grad, w_rest, w_rest, y_in, act, seq, state, gain, onehot)


def back_order(i):
    return jnp.where(i < 2, 2 + i, 3 - i)


def norm_kernel(
    inner_all, place, gate_ref, y_ref, gon_ref, stat, w_out, cm, cum, seq, gain, onehot,
    send, keep, out_in_ref, gy_ref, ggate_ref, gog, gstart, gin, gin_sum,
):
    step = pl.program_id(0)

    @pl.when(step == 0)
    def _():
        gog[...] = jnp.zeros_like(gog)
        gin_sum[...] = jnp.zeros_like(gin_sum)

    columns = jnp.transpose(jnp.concatenate([stat[...]] * (LANES // 8), axis=0))
    scale = lax.rsqrt(columns[:, 0:1] * (1.0 / inner_all) + EPSILON)
    along = columns[:, 1:2] * (1.0 / inner_all)
    gate, y, grad_on = gate_ref[...], y_ref[...], gon_ref[...]
    sig = sigmoid(gate)
    silu = gate * sig
    gated = y * silu
    normed = gated * scale
    out_in = (normed * gain[...]).astype(BF16)
    out_in_ref[...] = out_in
    mixed = dot_nt(out_in, w_out[...]).astype(BF16)

    @pl.when(step < 2)
    def _():
        send[...] = mixed

    @pl.when(step >= 2)
    def _():
        keep[...] = mixed

    gog[...] += fold_rows(grad_on * normed)
    grad_gated = scale * (grad_on * gain[...]) - gated * (scale * scale * scale * along)
    grad_y = (grad_gated * silu).astype(BF16)
    gy_ref[...] = grad_y
    ggate_ref[...] = (grad_gated * y * (sig * (1.0 + gate * (1.0 - sig)))).astype(BF16)
    hot = onehot[...]
    scaled = (grad_y.astype(F32) * by_heads(jnp.exp(cum[...]), hot)).astype(BF16)
    grad_start = dot_tn(cm[...], scaled)
    gstart[0] = grad_start
    rows = gate.shape[0]
    ahead = seq[rows - 1 : rows, :] - cum[rows - 1 : rows, :]
    gin_sum[...] += row_of(jnp.exp(ahead), hot) * grad_start
    gin[...] = gin_sum[...].astype(BF16)


def norm_stage(place, gate, y, grad_on, stat, w_rest, act, cum, seq, gain, onehot, inner_all):
    rows, inner = gate.shape
    dim = w_rest.shape[0]
    col = inner // LANES
    blocks = rows // CH
    at = lambda i, q: back_order(i) ^ q[0]
    block = pl.BlockSpec((CH, inner), lambda i, q: (at(i, q), 0))
    wide = pl.BlockSpec((CH, LANES), lambda i, q: (at(i, q), 0))
    low = jax.ShapeDtypeStruct((rows, inner), BF16)
    half = jax.ShapeDtypeStruct((rows // 2, dim), BF16)
    return pl.pallas_call(
        functools.partial(norm_kernel, inner_all),
        name="norm_stage",
        grid_spec=pltpu.PrefetchScalarGridSpec(
            num_scalar_prefetch=1,
            grid=(blocks,),
            in_specs=[
                block,
                block,
                block,
                pl.BlockSpec((8, CH), lambda i, q: (0, at(i, q))),
                pl.BlockSpec((dim, inner), lambda i, q: (0, 1)),
                pl.BlockSpec((CH, LANES), lambda i, q: (at(i, q), col + 1)),
                wide,
                wide,
                whole((1, inner)),
                whole((LANES, inner)),
            ],
            out_specs=[
                pl.BlockSpec((CH, dim), lambda i, q: (jnp.minimum(i, 1), 0)),
                pl.BlockSpec((CH, dim), lambda i, q: (jnp.minimum(3 - i, 1), 0)),
                block,
                block,
                block,
                whole((8, inner)),
                pl.BlockSpec((1, LANES, inner), lambda i, q: (at(i, q), 0, 0)),
                whole((LANES, inner)),
            ],
            scratch_shapes=[pltpu.VMEM((LANES, inner), F32)],
        ),
        out_shape=[
            half,
            half,
            low,
            low,
            low,
            jax.ShapeDtypeStruct((8, inner), F32),
            jax.ShapeDtypeStruct((blocks, LANES, inner), F32),
            jax.ShapeDtypeStruct((LANES, inner), BF16),
        ],
        compiler_params=params(),
        cost_estimate=cost(2 * rows * dim * inner, 18 * rows * inner + 4 * rows * dim, rows * inner),
    )(place, gate, y, grad_on, stat, w_rest, act, cum, seq, gain, onehot)


def early_kernel(grad_t, out_in, normed_t, ggate, out):
    inner = out_in.shape[1]
    out[:, 0:inner] = dot_nn(grad_t[...], out_in[...]).astype(BF16)
    out[:, inner:] = dot_nn(normed_t[...], ggate[...]).astype(BF16)


def early_grads(grad_t, out_in, normed_t, ggate):
    dim, rows = grad_t.shape
    inner = out_in.shape[1]
    tile = dim // 4
    return pl.pallas_call(
        early_kernel,
        name="early_grads",
        grid=(4,),
        in_specs=[
            pl.BlockSpec((tile, rows), lambda i: (i, 0)),
            whole((rows, inner)),
            pl.BlockSpec((tile, rows), lambda i: (i, 0)),
            whole((rows, inner)),
        ],
        out_specs=pl.BlockSpec((tile, 2 * inner), lambda i: (i, 0)),
        out_shape=jax.ShapeDtypeStruct((dim, 2 * inner), BF16),
        compiler_params=params(),
        cost_estimate=cost(4 * rows * dim * inner, 4 * dim * (rows + inner) + 4 * rows * inner, 0),
    )(grad_t, out_in, normed_t, ggate)


def lower_decay(mask, cum, cum_t, h):
    gap = jnp.where(mask, cum[:, h : h + 1] - cum_t[h : h + 1, :], 0.0)
    return jnp.where(mask, jnp.exp(gap), 0.0)


def scores_back_kernel(
    heads, xa_ref, bm_ref, cm_ref, gy_ref, dt_ref, cum_ref, seq_ref, cum_t_ref, last_ref,
    start_ref, in_state, gstart, gin, onehot, gbm_ref, gcm_ref, after_ref, after,
):
    step = pl.program_id(0)
    blocks = gstart.shape[0]
    hot = onehot[...]

    @pl.when(step == 0)
    def _():
        decays = by_heads(jnp.exp(last_ref[...]), hot)
        running = gin[...].astype(F32)
        for b in reversed(range(blocks)):
            after[b] = running
            running = gstart[b] + decays[b : b + 1, :] * running

    cum, cum_t = cum_ref[...], cum_t_ref[...]
    bm, cm, gy = bm_ref[...], cm_ref[...], gy_ref[...]
    rows = cum.shape[0]
    last = cum[rows - 1 : rows, :]
    ahead = seq_ref[rows - 1 : rows, :] - last
    start = start_ref[0] + row_of(jnp.exp(ahead), hot) * in_state[...].astype(F32)
    grad_after = after[step]
    after_ref[0] = grad_after
    x_dt = xa_ref[...].astype(F32) * by_heads(dt_ref[...], hot)
    x_low = x_dt.astype(BF16)
    mask = lax.broadcasted_iota(jnp.int32, (rows, rows), 0) >= lax.broadcasted_iota(jnp.int32, (rows, rows), 1)
    width = x_low.shape[1] // heads
    per = LANES // width
    lane = lax.broadcasted_iota(jnp.int32, (rows, LANES), 1) // width
    grad_scores = jnp.zeros((rows, rows), F32)
    for group in range(heads // per):
        at = slice(group * LANES, (group + 1) * LANES)
        x_group, gy_group = x_low[:, at], gy[:, at]
        for k in range(per):
            decay = lower_decay(mask, cum, cum_t, group * per + k)
            gy_head = jnp.where(lane == k, gy_group, jnp.zeros_like(gy_group))
            grad_scores = grad_scores + dot_nt(gy_head, x_group) * decay
    to_end = (x_dt * by_heads(jnp.exp(last - cum), hot)).astype(BF16)
    gy_scaled = (gy.astype(F32) * by_heads(jnp.exp(cum), hot)).astype(BF16)
    scores_low = grad_scores.astype(BF16)
    gbm_ref[...] = (dot_tn(scores_low, cm) + dot_nt(to_end, grad_after.astype(BF16))).astype(BF16)
    gcm_ref[...] = (dot_nn(scores_low, bm) + dot_nt(gy_scaled, start.astype(BF16))).astype(BF16)


def scores_backward(act, gy, dt, cum, seq, cum_t, lasts, starts, in_state, gstart, gin, onehot, heads):
    rows, inner = gy.shape
    col = inner // LANES
    blocks = rows // CH
    block = pl.BlockSpec((CH, inner), lambda b: (b, 0))
    wide = pl.BlockSpec((CH, LANES), lambda b: (b, 0))
    state = pl.BlockSpec((1, LANES, inner), lambda b: (b, 0, 0))
    return pl.pallas_call(
        functools.partial(scores_back_kernel, heads),
        name="scores_backward",
        grid=(blocks,),
        in_specs=[
            block,
            pl.BlockSpec((CH, LANES), lambda b: (b, col)),
            pl.BlockSpec((CH, LANES), lambda b: (b, col + 1)),
            block,
            wide,
            wide,
            wide,
            pl.BlockSpec((16, CH), lambda b: (0, b)),
            whole((8, LANES)),
            state,
            whole((LANES, inner)),
            whole((blocks, LANES, inner)),
            whole((LANES, inner)),
            whole((LANES, inner)),
        ],
        out_specs=[wide, wide, state],
        out_shape=[
            jax.ShapeDtypeStruct((rows, LANES), BF16),
            jax.ShapeDtypeStruct((rows, LANES), BF16),
            jax.ShapeDtypeStruct((blocks, LANES, inner), F32),
        ],
        scratch_shapes=[pltpu.VMEM((blocks, LANES, inner), F32)],
        compiler_params=params(),
        cost_estimate=cost(6 * rows * CH * inner, 10 * rows * inner, rows * CH * heads),
    )(act, act, act, gy, dt, cum, seq, cum_t, lasts, starts, in_state, gstart, gin, onehot)


def ssd_back_kernel(
    heads, offset, xa_ref, bm_ref, cm_ref, gy_ref, y_ref, dt_ref, sig_ref, cum_ref, seq_ref, cum_t_ref,
    start_ref, in_state, after_ref, pre_ref, taps, rate, skip, onehot, *rest,
):
    gconv_ref, graw_ref, head_ref, rows_sum, heads_sum, gx = rest[-6:]
    step = pl.program_id(0)
    hot = onehot[...]

    @pl.when(step == 0)
    def _():
        rows_sum[...] = jnp.zeros_like(rows_sum)
        heads_sum[...] = jnp.zeros_like(heads_sum)

    cum, cum_t, dt = cum_ref[...], cum_t_ref[...], dt_ref[...]
    bm, cm = bm_ref[...], cm_ref[...]
    rows = cum.shape[0]
    last = cum[rows - 1 : rows, :]
    ahead = seq_ref[rows - 1 : rows, :] - last
    start = start_ref[0] + row_of(jnp.exp(ahead), hot) * in_state[...].astype(F32)
    grad_after = after_ref[0]

    gy = gy_ref[...]
    xa = xa_ref[...].astype(F32)
    dt_wide = by_heads(dt, hot)
    x_dt = xa * dt_wide
    x_low = x_dt.astype(BF16)
    scores = dot_nt(cm, bm)
    mask = lax.broadcasted_iota(jnp.int32, (rows, rows), 0) >= lax.broadcasted_iota(jnp.int32, (rows, rows), 1)
    width = xa.shape[1] // heads
    per = LANES // width
    lane = lax.broadcasted_iota(jnp.int32, (rows, LANES), 1) // width
    for group in range(heads // per):
        at = slice(group * LANES, (group + 1) * LANES)
        gy_group = gy[:, at]
        total = jnp.zeros((rows, LANES), F32)
        for k in range(per):
            weights = (lower_decay(mask, cum, cum_t, group * per + k) * scores).astype(BF16)
            total = total + dot_tn(weights, jnp.where(lane == k, gy_group, jnp.zeros_like(gy_group)))
        gx[:, at] = total

    end_wide = by_heads(jnp.exp(last - cum), hot)
    from_end = dot_nn(bm, grad_after.astype(BF16))
    to_end = (x_dt * end_wide).astype(BF16)
    gx_intra = gx[...]
    gx_all = gx_intra + end_wide * from_end
    end_term = to_end.astype(F32) * from_end
    gy_f = gy.astype(F32)
    grad_xa = dt_wide * gx_all + skip[...] * gy_f

    grad_dt = by_heads_t(xa * gx_all, hot)
    grad_cum = by_heads_t(
        gy_f * (y_ref[...] - skip[...] * xa) - x_low.astype(F32) * gx_intra - end_term, hot
    )
    end_rows = fold_rows(end_term)
    state_rows = fold_rows(grad_after * start) * row_of(jnp.exp(last), hot)
    grad_last = jnp.sum(by_heads_t(end_rows + state_rows, hot), axis=0, keepdims=True)
    upper = (
        lax.broadcasted_iota(jnp.int32, (rows, rows), 0) <= lax.broadcasted_iota(jnp.int32, (rows, rows), 1)
    ).astype(BF16)
    grad_a = jnp.broadcast_to(grad_last, grad_cum.shape)
    for part in exact_parts(grad_cum):
        grad_a = grad_a + dot_nn(upper, part)
    grad_raw = (grad_dt + rate[...] * grad_a) * sig_ref[...]
    graw_ref[...] = grad_raw.astype(BF16)
    heads_sum[0:8, :] += fold_rows(grad_raw)
    heads_sum[8:16, :] += fold_rows(grad_a * dt * rate[...])

    tap_count = 4
    first = HALO - tap_count + 1
    base = pl.multiple_of((step + offset) * rows, rows)
    window = pre_ref[pl.ds(base, rows + HALO), :]
    conv = taps[tap_count : tap_count + 1, :] + taps[0:1, :] * window[first : first + rows]
    for k in range(1, tap_count):
        conv = conv + taps[k : k + 1, :] * window[first + k : first + k + rows]
    sig = sigmoid(conv)
    gconv = grad_xa * (sig * (1.0 + conv * (1.0 - sig)))
    gconv_ref[...] = gconv

    @pl.when(step == 0)
    def _():
        head_ref[...] = gconv[0:HALO, :]

    for k in range(tap_count):
        rows_sum[8 * k : 8 * k + 8, :] += fold_rows(gconv * window[first + k : first + k + rows])
    rows_sum[8 * tap_count : 8 * tap_count + 8, :] += fold_rows(gconv)
    rows_sum[8 * tap_count + 8 : 8 * tap_count + 16, :] += fold_rows(gy_f * xa)


def ssd_backward(
    act, gy, y, dt, sig, cum, seq, cum_t, starts, in_state, after, pre, taps, rate, skip, onehot, heads,
    offset, count, into,
):
    rows, inner = gy.shape
    col = inner // LANES
    block = pl.BlockSpec((CH, inner), lambda b: (b + offset, 0))
    wide = pl.BlockSpec((CH, LANES), lambda b: (b + offset, 0))
    state = pl.BlockSpec((1, LANES, inner), lambda b: (b + offset, 0, 0))
    operands = [act, act, act, gy, y, dt, sig, cum, seq, cum_t, starts, in_state, after, pre, taps, rate, skip, onehot]
    specs = [
        block,
        pl.BlockSpec((CH, LANES), lambda b: (b + offset, col)),
        pl.BlockSpec((CH, LANES), lambda b: (b + offset, col + 1)),
        block,
        block,
        wide,
        wide,
        wide,
        wide,
        pl.BlockSpec((16, CH), lambda b: (0, b + offset)),
        state,
        whole((LANES, inner)),
        state,
        pl.BlockSpec((rows + HALO, inner), lambda b: (0, 0)),
        pl.BlockSpec((8, inner), lambda b: (0, 0)),
        whole((1, LANES)),
        whole((1, inner)),
        whole((LANES, inner)),
    ]
    aliases = {}
    if into is not None:
        aliases = {len(operands): 0, len(operands) + 1: 1}
        operands += list(into)
        specs += [pl.BlockSpec(memory_space=pl.ANY)] * 2
    part = CH * count
    return pl.pallas_call(
        functools.partial(ssd_back_kernel, heads, offset),
        name="ssd_backward",
        grid=(count,),
        in_specs=specs,
        out_specs=[block, wide, whole((HALO, inner)), whole((48, inner)), whole((16, LANES))],
        out_shape=[
            jax.ShapeDtypeStruct((rows, inner), F32),
            jax.ShapeDtypeStruct((rows, LANES), BF16),
            jax.ShapeDtypeStruct((HALO, inner), F32),
            jax.ShapeDtypeStruct((48, inner), F32),
            jax.ShapeDtypeStruct((16, LANES), F32),
        ],
        input_output_aliases=aliases,
        scratch_shapes=[pltpu.VMEM((CH, inner), F32)],
        compiler_params=params(),
        cost_estimate=cost(8 * part * CH * inner, 24 * part * inner, part * CH * heads),
    )(*operands)


def bc_kernel(side, grad, pre_ref, taps, gconv_ref, tap_sum):
    tap_count = 4
    rows = grad.shape[0]
    first = HALO - tap_count + 1
    conv = taps[tap_count : tap_count + 1, :] + taps[0:1, :] * pre_ref[first : first + rows, :]
    for k in range(1, tap_count):
        conv = conv + taps[k : k + 1, :] * pre_ref[first + k : first + k + rows, :]
    sig = sigmoid(conv)
    gconv = grad[...] * (sig * (1.0 + conv * (1.0 - sig)))
    gconv_ref[...] = gconv
    for k in range(tap_count):
        tap_sum[8 * k : 8 * k + 8, :] = fold_rows(gconv * pre_ref[first + k : first + k + rows, :])
    tap_sum[8 * tap_count : 8 * tap_count + 8, :] = fold_rows(gconv)


def bc_backward(side, grad, pre, taps, col):
    rows = grad.shape[0]
    return pl.pallas_call(
        bc_kernel,
        name="bc_backward",
        grid_spec=pltpu.PrefetchScalarGridSpec(
            num_scalar_prefetch=1,
            grid=(1,),
            in_specs=[
                pl.BlockSpec((rows, LANES), lambda i, s: (0, 0)),
                pl.BlockSpec((rows + HALO, LANES), lambda i, s: (0, col + s[0])),
                pl.BlockSpec((8, LANES), lambda i, s: (0, col + s[0])),
            ],
            out_specs=[
                pl.BlockSpec((rows, LANES), lambda i, s: (0, 0)),
                pl.BlockSpec((40, LANES), lambda i, s: (0, 0)),
            ],
        ),
        out_shape=[
            jax.ShapeDtypeStruct((rows, LANES), F32),
            jax.ShapeDtypeStruct((40, LANES), F32),
        ],
        compiler_params=params(),
        cost_estimate=cost(30 * rows * LANES, 16 * rows * LANES, rows * LANES),
    )(side, grad, pre, taps)


def conv_transpose(grad_ref, next_ref, halo_ref, taps, ext, at_end):
    tap_count = 4
    rows = grad_ref.shape[0]
    ext[0:rows, :] = grad_ref[...]
    ext[rows:, :] = jnp.where(at_end, halo_ref[...], next_ref[...])
    total = taps[tap_count - 1 : tap_count, :] * ext[0:rows, :]
    for k in range(tap_count - 1):
        ahead = tap_count - 1 - k
        total = total + taps[k : k + 1, :] * ext[ahead : ahead + rows, :]
    return total.astype(BF16)


def input_kernel(
    share, where, gx_ref, gx_next, gx_halo, gb_ref, gb_next, gb_halo, taps_x, taps_b, ggate, graw,
    w_gate, w_x, w_b, w_dt, send, keep, gcat_a, gcat_b, ext_x, ext_b,
):
    step = pl.program_id(0)
    at_end = (back_order(step) ^ where[0]) == pl.num_programs(0) - 1
    gpre_x = conv_transpose(gx_ref, gx_next, gx_halo, taps_x, ext_x, at_end)
    gpre_b = conv_transpose(gb_ref, gb_next, gb_halo, taps_b, ext_b, at_end)
    cut = gcat_a.shape[1]
    gcat_a[...] = gpre_x[:, :cut]
    rest = gpre_x.shape[1] - cut
    gcat_b[:, 0:rest] = gpre_x[:, cut:]
    gcat_b[:, rest:] = gpre_b
    total = dot_nt(ggate[...], w_gate[...]) + dot_nt(gpre_x, w_x[...])
    total = total + dot_nt(graw[...], w_dt[...]) + share * dot_nt(gpre_b, w_b[...])
    part = total.astype(BF16)

    @pl.when(step < 2)
    def _():
        send[...] = part

    @pl.when(step >= 2)
    def _():
        keep[...] = part


def input_stage(where, gx, gx_halo, gb, gb_halo, taps, ggate, graw, w_rest, w_first, share):
    rows, inner = gx.shape
    dim = w_rest.shape[0]
    col = inner // LANES
    per = CH // HALO
    top = rows // HALO - 1
    blocks = rows // CH
    at = lambda i, q: back_order(i) ^ q[0]
    nxt = lambda i, q: (jnp.minimum(per * (at(i, q) + 1), top), 0)
    cut = 4 * LANES
    half = jax.ShapeDtypeStruct((rows // 2, dim), BF16)
    return pl.pallas_call(
        functools.partial(input_kernel, share),
        name="input_stage",
        grid_spec=pltpu.PrefetchScalarGridSpec(
            num_scalar_prefetch=1,
            grid=(blocks,),
            in_specs=[
                pl.BlockSpec((CH, inner), lambda i, q: (at(i, q), 0)),
                pl.BlockSpec((HALO, inner), nxt),
                pl.BlockSpec((HALO, inner), lambda i, q: (0, 0)),
                pl.BlockSpec((CH, LANES), lambda i, q: (at(i, q), 0)),
                pl.BlockSpec((HALO, LANES), nxt),
                pl.BlockSpec((HALO, LANES), lambda i, q: (0, 0)),
                pl.BlockSpec((8, inner), lambda i, q: (0, 0)),
                pl.BlockSpec((8, LANES), lambda i, q: (0, col + q[1])),
                pl.BlockSpec((CH, inner), lambda i, q: (at(i, q), 0)),
                pl.BlockSpec((CH, LANES), lambda i, q: (at(i, q), 0)),
                pl.BlockSpec((dim, inner), lambda i, q: (0, 0)),
                pl.BlockSpec((dim, inner), lambda i, q: (0, 0)),
                pl.BlockSpec((dim, LANES), lambda i, q: (0, col + q[1])),
                pl.BlockSpec((dim, LANES), lambda i, q: (0, col + 2)),
            ],
            out_specs=[
                pl.BlockSpec((CH, dim), lambda i, q: (jnp.minimum(i, 1), 0)),
                pl.BlockSpec((CH, dim), lambda i, q: (jnp.minimum(3 - i, 1), 0)),
                pl.BlockSpec((CH, cut), lambda i, q: (at(i, q), 0)),
                pl.BlockSpec((CH, inner + LANES - cut), lambda i, q: (at(i, q), 0)),
            ],
            scratch_shapes=[pltpu.VMEM((CH + HALO, inner), F32), pltpu.VMEM((CH + HALO, LANES), F32)],
        ),
        out_shape=[
            half,
            half,
            jax.ShapeDtypeStruct((rows, cut), BF16),
            jax.ShapeDtypeStruct((rows, inner + LANES - cut), BF16),
        ],
        compiler_params=params(),
        cost_estimate=cost(4 * rows * dim * inner, 10 * rows * inner + 2 * rows * dim, 0),
    )(where, gx, gx, gx_halo, gb, gb, gb_halo, taps, taps, ggate, graw, w_rest, w_first, w_first, w_first)


def late_kernel(side, normed_t, gcat, keep, send):
    result = dot_nn(normed_t[...], gcat[...]).astype(BF16)
    rows = result.shape[0] // 2
    top, bottom = result[:rows], result[rows:]
    first = side[0] == 0
    keep[0] = jnp.where(first, top, bottom)
    send[0] = jnp.where(first, bottom, top)


def late_grads(side, normed_t, gcat, shards):
    dim, rows = normed_t.shape
    width = gcat.shape[1]
    tile = dim // shards
    half = pl.BlockSpec((1, tile // 2, width), lambda i, q: (i, 0, 0))
    shape = jax.ShapeDtypeStruct((shards, tile // 2, width), BF16)
    return pl.pallas_call(
        late_kernel,
        name="late_grads",
        grid_spec=pltpu.PrefetchScalarGridSpec(
            num_scalar_prefetch=1,
            grid=(shards,),
            in_specs=[
                pl.BlockSpec((tile, rows), lambda i, q: (i, 0)),
                pl.BlockSpec((rows, width), lambda i, q: (0, 0)),
            ],
            out_specs=[half, half],
        ),
        out_shape=[shape, shape],
        compiler_params=params(),
        cost_estimate=cost(2 * rows * dim * width, 2 * dim * (rows + width) + 2 * rows * width, 0),
    )(side, normed_t, gcat)


def on_device(
    hidden_in,
    norm_gain,
    w_in_zx,
    w_in_bc,
    w_in_dt,
    conv_x,
    conv_bc,
    dt_bias,
    a_log,
    d_skip,
    out_gain,
    w_out,
    cotangent,
):
    seq_count, rows, dim = hidden_in.shape
    inner = w_in_zx.shape[2]
    heads = w_in_dt.shape[1]
    head_dim = inner // heads
    tap_count = conv_x.shape[0] - 1
    tensor_size, shards, contexts = lax.axis_size("tensor"), lax.axis_size("shard"), lax.axis_size("context")
    inner_all = inner * tensor_size
    blocks = rows // CH
    assert seq_count == 1 and tensor_size == 4 and blocks == 4 and contexts == 2
    shard_rows = w_in_zx.shape[0]
    place = lax.axis_index("tensor")
    context = lax.axis_index("context")
    side_num = place % 2
    quarter = side_num * 2 + place // 2
    where = jnp.stack([quarter, side_num]).astype(jnp.int32)
    col = inner // LANES

    x_rows = hidden_in.reshape(rows, dim)
    g_rows = cotangent.reshape(rows, dim)

    pad_dt = jnp.zeros((shard_rows, LANES - heads), BF16)
    w_front = jnp.concatenate([w_in_zx[:, 1], w_in_bc, w_in_dt, pad_dt], axis=1)
    w_back = jnp.concatenate([w_in_zx[:, 0], w_out.T], axis=1)
    half_rows = shard_rows // contexts
    w_rest = lax.all_gather(
        lax.dynamic_slice_in_dim(w_back, context * half_rows, half_rows, 0), ("shard", "context"), axis=0, tiled=True
    )
    w_first = gather_weights(w_front)
    halo_rows = shifted(x_rows[rows - HALO :], "context", 1)

    def norm_of(values):
        wide = values.astype(F32)
        scale = lax.rsqrt(jnp.mean(wide * wide, axis=-1, keepdims=True) + EPSILON)
        return (wide * scale * norm_gain).astype(BF16)

    normed = norm_of(x_rows)
    halo = norm_of(halo_rows)
    normed_t = normed.T
    grad_t = g_rows.T

    pad_heads = lambda v: jnp.pad(v, (0, LANES - heads)).reshape(1, LANES)
    rate = pad_heads(-jnp.exp(a_log))
    bias = pad_heads(dt_bias)
    skip = jnp.repeat(d_skip, head_dim).reshape(1, inner)
    gain = out_gain.reshape(1, inner)
    taps = jnp.pad(jnp.concatenate([conv_x, conv_bc], axis=1), ((0, 8 - tap_count - 1), (0, 0)))
    onehot = (
        lax.broadcasted_iota(jnp.int32, (LANES, inner), 0)
        == lax.broadcasted_iota(jnp.int32, (LANES, inner), 1) // head_dim
    ).astype(BF16)

    dt, sig, cum, seq, cum_t = step_sizes(normed, w_first, bias, rate, col + 2)
    act, pre = conv_front(normed, halo, w_first, taps)
    y_local, starts, end_state = ssd_forward(act, dt, cum, cum_t, skip, onehot, heads)
    lasts = jnp.pad(cum.reshape(blocks, CH, LANES)[:, CH - 1], ((0, 8 - blocks), (0, 0)))
    in_state = shifted(end_state.astype(BF16), "context", 1)

    gate, y, grad_on, stat = gate_stage(normed, g_rows, w_rest, y_local, act, seq, in_state, gain, onehot)
    stat = butterfly(stat, "tensor")
    send, keep, out_in, gy, ggate, gog, gstart, gin_first = norm_stage(
        where, gate, y, grad_on, stat, w_rest, act, cum, seq, gain, onehot, inner_all
    )
    gin = shifted(gin_first, "context", -1)

    early = early_grads(grad_t, out_in, normed_t, ggate)
    early_share = lax.psum_scatter(early, ("shard", "context"), scatter_dimension=0, tiled=True).astype(F32)

    mixed_mine = reduce_mine(keep, send, tensor_size)
    own_rows = rows // 4
    x_mine = lax.dynamic_slice_in_dim(x_rows, quarter * own_rows, own_rows, 0).astype(F32)
    stream_mine = x_mine + mixed_mine
    square_sums = jnp.stack([jnp.sum(stream_mine * stream_mine), jnp.sum(mixed_mine * mixed_mine)])
    out = gather_quarters(stream_mine.astype(BF16), where, tensor_size, BF16)

    gy, gin, early = lax.optimization_barrier((gy, gin, early))
    gbm, gcm, after = scores_backward(
        act, gy, dt, cum, seq, cum_t, lasts, starts, in_state, gstart, gin, onehot, heads
    )
    core_send = jnp.where(side_num == 0, gcm, gbm)
    core_keep = jnp.where(side_num == 0, gbm, gcm)
    core_got = lax.ppermute(core_send, "tensor", swap_pairs(tensor_size, 1))
    state = (act, gy, y, dt, sig, cum, seq, cum_t, starts, in_state, after, pre, taps, rate, skip, onehot, heads)
    gconv, graw, head, rows_sum_a, heads_sum_a = ssd_backward(*state, 0, 2, None)
    gx_halo = shifted(head, "context", -1)
    core_got, gconv = lax.optimization_barrier((core_got, gconv))
    chip_low = (core_keep.astype(F32) + core_got.astype(F32)).astype(BF16)
    chip_got = lax.ppermute(chip_low, "tensor", swap_pairs(tensor_size, 2))
    gconv, chip_low = lax.optimization_barrier((gconv, chip_low))
    gconv, graw, _, rows_sum_b, heads_sum_b = ssd_backward(*state, 2, 2, (gconv, graw))
    bc_sum = chip_low.astype(F32) + chip_got.astype(F32)
    gconv_bc, tap_bc = bc_backward(where[1:], bc_sum, pre, taps, col)
    gb_halo = shifted(gconv_bc[:HALO], "context", -1)

    send, keep, gcat_a, gcat_b = input_stage(
        where, gconv, gx_halo, gconv_bc, gb_halo, taps, ggate, graw, w_rest, w_first, 2.0 / tensor_size
    )
    if shards <= 8:
        context_num = context.astype(jnp.int32).reshape(1)
        late_share = [
            scatter_grad(*late_grads(context_num, normed_t, piece, shards)) for piece in (gcat_a, gcat_b)
        ]
    else:
        late_share = [
            lax.psum_scatter(
                dot_nn(normed_t, piece).astype(BF16), ("shard", "context"), scatter_dimension=0, tiled=True
            ).astype(F32)
            for piece in (gcat_a, gcat_b)
        ]
    cut = inner - gcat_a.shape[1]

    grad_normed = reduce_mine(keep, send, tensor_size)
    scale_mine = lax.rsqrt(jnp.mean(x_mine * x_mine, axis=-1, keepdims=True) + EPSILON)
    g_mine = lax.dynamic_slice_in_dim(g_rows, quarter * own_rows, own_rows, 0).astype(F32)
    grad_ng = jnp.sum(grad_normed * x_mine * scale_mine, axis=0)
    grad_un = grad_normed * norm_gain
    grad_mine = (
        g_mine
        + scale_mine * grad_un
        - x_mine * scale_mine**3 * jnp.mean(grad_un * x_mine, axis=-1, keepdims=True)
    )
    grad_input = gather_quarters(grad_mine.astype(BF16), where, tensor_size, F32)

    grad_dt_t = dot_tn(graw[:, :16], normed)
    local = jnp.concatenate(
        [
            grad_dt_t.reshape(-1, inner),
            (rows_sum_a + rows_sum_b).reshape(6, 8, inner).sum(1),
            gog.sum(0, keepdims=True),
            jnp.pad((heads_sum_a + heads_sum_b).reshape(2, 8, LANES).sum(1), ((0, 0), (0, inner - LANES))),
        ],
        axis=0,
    )
    local = butterfly(butterfly(local, "context"), "shard")
    first = 16 * dim // inner
    grad_dt_all = local[:first].reshape(16, dim)
    local = local[first:]

    own_taps = jnp.pad(tap_bc.reshape(tap_count + 1, 8, LANES).sum(1), ((0, 3), (0, 0))) * (2.0 / tensor_size)
    nothing = jnp.zeros_like(own_taps)
    shared = jnp.concatenate(
        [
            grad_ng.reshape(-1, 2 * LANES),
            jnp.concatenate(
                [jnp.where(side_num == 0, own_taps, nothing), jnp.where(side_num == 0, nothing, own_taps)], axis=1
            ),
            jnp.pad(square_sums.reshape(1, 2), ((0, 7), (0, 2 * LANES - 2))),
        ],
        axis=0,
    )
    shared = butterfly(butterfly(butterfly(shared, "tensor"), "context"), "shard")
    ng_rows = dim // (2 * LANES)
    totals = shared[ng_rows + 8]
    entry_count = rows * dim * shards * contexts

    bc_mine = late_share[1][:, cut:]
    bc_other = lax.ppermute(bc_mine, "tensor", swap_pairs(tensor_size, 1))
    grad_wbc = jnp.concatenate(
        [jnp.where(side_num == 0, bc_mine, bc_other), jnp.where(side_num == 0, bc_other, bc_mine)], axis=1
    )
    own_features = (lax.axis_index("shard") * contexts + context) * half_rows
    return (
        out.reshape(hidden_in.shape),
        grad_input.reshape(hidden_in.shape),
        shared[:ng_rows].reshape(dim),
        jnp.stack(
            [early_share[:, inner:], jnp.concatenate([late_share[0], late_share[1][:, :cut]], axis=1)], axis=1
        ),
        grad_wbc,
        lax.dynamic_slice_in_dim(grad_dt_all, own_features, half_rows, 1)[:heads].T,
        local[: tap_count + 1],
        shared[ng_rows : ng_rows + tap_count + 1],
        local[tap_count + 3, :heads],
        local[tap_count + 4, :heads],
        local[tap_count + 1].reshape(heads, head_dim).sum(1),
        local[tap_count + 2],
        early_share[:, :inner].T,
        jnp.sqrt(totals[0] / entry_count),
        jnp.sqrt(totals[1] / entry_count),
    )


def solution(mesh):
    placed = (
        P("shard", "context", None),
        P(),
        P("shard", None, "tensor"),
        P("shard", None),
        P("shard", "tensor"),
        P(None, "tensor"),
        P(),
        P("tensor"),
        P("tensor"),
        P("tensor"),
        P("tensor"),
        P("tensor", "shard"),
        P("shard", "context", None),
    )
    return jax.shard_map(
        on_device,
        mesh=mesh,
        in_specs=placed,
        out_specs=(
            P("shard", "context", None),
            P("shard", "context", None),
            P(),
            P(("shard", "context"), None, "tensor"),
            P(("shard", "context"), None),
            P(("shard", "context"), "tensor"),
            P(None, "tensor"),
            P(),
            P("tensor"),
            P("tensor"),
            P("tensor"),
            P("tensor"),
            P("tensor", ("shard", "context")),
            P(),
            P(),
        ),
        check_vma=False,
    )
```

time: 1060 us -> 463 us (0.44)
  waiting for transfers between devices: 565 us -> 112 us
  Pallas kernels: 0 us -> 145 us
  blocking collectives: 125 us -> 0 us
  matrix products: 111 us -> 1.92 us
  starting transfers between devices: 5.28 us -> 86.9 us
  local copies, waits for them, and re-layouts: 125 us -> 51.8 us
  other arithmetic: 99.2 us -> 38.2 us
    reduce_scatter x3 -> x1, waiting for transfers between devices: 267 us -> 0.01 us  [on_device(): lax.psum_scatter(early, ('shard', 'context'), scatter_dimension=0, tiled=...]
    psum x2 -> x0, waiting for transfers between devices: 247 us -> none  [the longest x1 221 us: on_device(): lax.psum(jnp.dot(out_in, out_full, preferred_element_type=jnp.float32), '...]
    pallas_call x0 -> x15, Pallas kernels: none -> 145 us  [the longest x2 34 us: ssd_backward(): pl.pallas_call(functools.partial(ssd_back_kernel, heads, offset), name='s...]
    ppermute x0 -> x49, waiting for transfers between devices: none -> 109 us  [the longest x10 39 us: butterfly(): value = value + lax.ppermute(value, axis, swap_pairs(size, by))]
    dot_general x22 -> x1, matrix products: 108 us -> 1.92 us  [dot_tn(): lax.dot_general(a, b, (((0,), (0,)), ((), ())), preferred_element_type=F32)]
    ppermute x0 -> x49, starting transfers between devices: none -> 75.1 us  [the longest x6 27.6 us: scatter_grad(): plus = lax.ppermute(up, 'shard', [(i, i + 1) for i in range(k)])]
    all_gather x4 -> x0, blocking collectives: 65.7 us -> none  [the longest x1 29.5 us: on_device(): lax.all_gather(w_in_bc, 'shard', axis=0, tiled=True)]
    psum x3 -> x0, blocking collectives: 53.5 us -> none  [the longest x1 41.1 us: on_device(): lax.psum((grad_ng, grad_taps[:, :inner_dev], grad_taps[:, inner_dev:], gr...]
  transfers between devices with their start and end apart: 10 -> 56, of which waited for: 7 -> 17; matrix products, arithmetic and copies ran while one was open for 20% -> 17% of each run, Pallas kernels for 0% -> 23%
where the time goes in v1:
time: 463 us; the launch traced here: 455 us
  Pallas kernels  145 us (31%)
  waiting for transfers between devices  112 us (24%)
  starting transfers between devices  86.9 us (19%)
  local copies, waits for them, and re-layouts  51.8 us (11%)
  other arithmetic  38.2 us (8%)
  between operations  18.9 us (4%)
    ppermute x10, waiting for transfers between devices, butterfly(): value = value + lax.ppermute(value, axis, swap_pairs(size, by))  39 us
    pallas_call x2, Pallas kernels, ssd_backward(): pl.pallas_call(functools.partial(ssd_back_kernel, heads, offset), name='s...  34 us
    ppermute x3, waiting for transfers between devices, gather_weights(): lax.ppermute(minus, axes, joint_pairs(shards, parts, range(1, shards - k...  30 us
    ppermute x6, starting transfers between devices, scatter_grad(): plus = lax.ppermute(up, 'shard', [(i, i + 1) for i in range(k)])  27.6 us
    unnamed x99, local copies, waits for them, and re-layouts  17.5 us
    ppermute x2, waiting for transfers between devices, scatter_grad(): got = lax.ppermute(send, 'context', swap_pairs(2, 1))  16.7 us
    pallas_call x1, Pallas kernels, input_stage(): pl.pallas_call(functools.partial(input_kernel, share), name='input_stage'...  14.1 us
    pallas_call x1, Pallas kernels, norm_stage(): pl.pallas_call(functools.partial(norm_kernel, inner_all), name='norm_stag...  13.9 us
  transfers between devices with their start and end apart: 56, of which 17 were waited for; matrix products, arithmetic and copies ran while one was open for 17% of the time, Pallas kernels for 23%

profile of v1, /device:TPU:0, one launch (start us, length us, event | category | flops | bytes accessed | tf_op | source)
XLA Modules:
  0.0 454.7 jit_solution(2039927878548644712)
XLA Ops:
  14.7 6.4 %collective-permute-start.1 = (bf16[192,1152]{1,0:T(8,128)(2,1)}, bf16[192,1152]{1,0:T(8,128)(2,1)}, u32[]{:S(2)}, u32[]{:S(2)}) collective-permute-start(bf16[192,1152]{1,0:T(8,128)(2,1)} %constant_dynamic-slice_fusion), channel_id=1, source_target_pairs={{0,8},{4,12},{8,16},{12,20},{16,24},{20,28},{1,9},{5,13},{9,17},{1... | collective-permute-start | bytes 1327112 | tf_op jit(solution)/shard_map/ppermute | solution.py:61
  21.9 4.0 collective-permute-start
  25.8 3.2 copy.41
  31.7 2.3 broadcast_in_dim.10
  34.9 2.4 fusion.2
  38.6 4.7 %copy.49.normed = bf16[1024,1536]{1,0:T(8,128)(2,1)} copy(bf16[1024,1536]{0,1:T(8,128)(2,1)} %fusion.2) | data formatting | bytes 6291456 | tf_op jit(solution)/shard_map/convert_element_type | solution.py:968
  52.4 5.2 %collective-permute-done.6 = bf16[192,1152]{1,0:T(8,128)(2,1)S(1)} collective-permute-done((bf16[192,1152]{1,0:T(8,128)(2,1)}, bf16[192,1152]{1,0:T(8,128)(2,1)S(1)}, u32[]{:S(2)}, u32[]{:S(2)}) %collective-permute-start.6) | collective-permute-done | bytes 442400 | tf_op jit(solution)/shard_map/ppermute | solution.py:62
  58.8 3.2 collective-permute-start.8
  66.7 24.8 %collective-permute-done.10 = bf16[192,1152]{1,0:T(8,128)(2,1)S(1)} collective-permute-done((bf16[192,1152]{1,0:T(8,128)(2,1)S(1)}, bf16[192,1152]{1,0:T(8,128)(2,1)S(1)}, u32[]{:S(2)}, u32[]{:S(2)}) %collective-permute-start.10) | collective-permute-done | bytes 442400 | tf_op jit(solution)/shard_map/ppermute | solution.py:62
  91.4 3.3 collective-permute-start.12
  99.5 5.2 %collective-permute-done.12 = bf16[192,1152]{1,0:T(8,128)(2,1)S(1)} collective-permute-done((bf16[192,1152]{1,0:T(8,128)(2,1)S(1)}, bf16[192,1152]{1,0:T(8,128)(2,1)S(1)}, u32[]{:S(2)}, u32[]{:S(2)}) %collective-permute-start.12) | collective-permute-done | bytes 442400 | tf_op jit(solution)/shard_map/ppermute | solution.py:64
  105.5 5.5 %step_sizes.1 = (f32[1024,128]{1,0:T(8,128)}, f32[1024,128]{1,0:T(8,128)}, f32[1024,128]{1,0:T(8,128)}, f32[1024,128]{1,0:T(8,128)}, f32[16,1024]{1,0:T(8,128)}) custom-call(bf16[1024,1536]{1,0:T(8,128)(2,1)} %copy.49.normed, bf16[1728,1152]{1,0:T(8,128)(2,1)} %constant_dynamic-update-slice_fusion.weight.w_x.w_b.w_dt, f32[1,128]{1,0:T(1,128)} %pad_bitcast_fusion.1.bias, ...), custom_call_target="tpu_custom_call" | custom-call | flops 402653184 | bytes 5767168 | tf_op jit(solution)/shard_map/step_sizes/pallas_call | solution.py:256
  110.9 11.0 %conv_front.1 = (bf16[1024,1024]{1,0:T(8,128)(2,1)}, f32[1032,1024]{1,0:T(8,128)}) custom-call(bf16[1024,1536]{1,0:T(8,128)(2,1)} %copy.49.normed, bf16[8,1536]{1,0:T(8,128)(2,1)} %fusion.27.halo, bf16[1728,1152]{1,0:T(8,128)(2,1)} %constant_dynamic-update-slice_fusion.weight.w_x.w_b.w_dt, f32[8,1024]{1,0:T(8,128)} %select_maximum_fusion.1.taps.taps_x.taps_b), custom_call_target="tpu_custom_call" | custom-call | flops 3221225472 | bytes 12582912 | tf_op jit(solution)/shard_map/conv_front/pallas_call | solution.py:206
  121.9 9.3 %ssd_forward.1 = (f32[1024,768]{1,0:T(8,128)}, f32[4,128,768]{2,1,0:T(8,128)}, f32[128,768]{1,0:T(8,128)}) custom-call(bf16[1024,1024]{1,0:T(8,128)(2,1)} %get-tuple-element.65.xa_ref.bm_ref.cm_ref.cm, bf16[1024,1024]{1,0:T(8,128)(2,1)} %get-tuple-element.65.xa_ref.bm_ref.cm_ref.cm, bf16[1024,1024]{1,0:T(8,128)(2,1)} %get-tuple-element.65.xa_ref.bm_ref.cm_ref.cm, ...), custom_call_target="tpu_custom_call" | custom-call | flops 1207959552 | bytes 9437184 | tf_op jit(solution)/shard_map/ssd_forward/pallas_call | solution.py:316
  132.2 3.9 collective-permute-start.13
  136.7 2.3 collective-permute-done.13.state.in_state
  139.7 13.1 %gate_stage.1 = (f32[1024,768]{1,0:T(8,128)}, f32[1024,768]{1,0:T(8,128)}, f32[1024,768]{1,0:T(8,128)}, f32[8,1024]{1,0:T(8,128)}) custom-call(bf16[1024,1536]{1,0:T(8,128)(2,1)} %copy.49.normed, bf16[1024,1536]{1,0:T(8,128)(2,1)} %bitcast.108, bf16[1536,1536]{1,0:T(8,128)(2,1)} %all-gather.2.cloned.1.call-done.w_gate.w_out, ...), custom_call_target="tpu_custom_call" | custom-call | flops 4831838208 | bytes 18874368 | tf_op jit(solution)/shard_map/gate_stage/pallas_call | solution.py:367
  153.0 2.4 fusion.38.normed_t
  157.5 4.7 %copy.42 = bf16[1,1024,1536]{1,2,0:T(8,128)(2,1)} copy(bf16[1,1024,1536]{2,1,0:T(8,128)(2,1)} %param.25) | data formatting | bytes 6291456 | tf_op args[12]
  164.1 13.9 %norm_stage.1 = (bf16[512,1536]{1,0:T(8,128)(2,1)}, bf16[512,1536]{1,0:T(8,128)(2,1)}, bf16[1024,768]{1,0:T(8,128)(2,1)}, bf16[1024,768]{1,0:T(8,128)(2,1)}, bf1...) custom-call(s32[2]{0:T(128)} %pad_add_fusion.place.where, ...), custom_call_target="tpu_custom_call" | custom-call | flops 2415919104 | bytes 20447232 | tf_op jit(solution)/shard_map/norm_stage/pallas_call | solution.py:450
  179.3 9.5 %early_grads.1 = bf16[1536,1536]{1,0:T(8,128)(2,1)} custom-call(bf16[1536,1024]{1,0:T(8,128)(2,1)} %bitcast.112, bf16[1024,768]{1,0:T(8,128)(2,1)} %get-tuple-element.80.out_in, bf16[1536,1024]{1,0:T(8,128)(2,1)} %fusion.38.normed_t, bf16[1024,768]{1,0:T(8,128)(2,1)} %get-tuple-element.81.ggate), custom_call_target="tpu_custom_call" | custom-call | flops 4831838208 | bytes 14155776 | tf_op jit(solution)/shard_map/early_grads/pallas_call | solution.py:505
  189.5 11.4 %scores_backward.1 = (bf16[1024,128]{1,0:T(8,128)(2,1)}, bf16[1024,128]{1,0:T(8,128)(2,1)}, f32[4,128,768]{2,1,0:T(8,128)}) custom-call(bf16[1024,1024]{1,0:T(8,128)(2,1)} %get-tuple-element.65.xa_ref.bm_ref.cm_ref.cm, bf16[1024,1024]{1,0:T(8,128)(2,1)} %get-tuple-element.65.xa_ref.bm_ref.cm_ref.cm, ...), custom_call_target="tpu_custom_call" | custom-call | flops 1207959552 | bytes 7864320 | tf_op jit(solution)/shard_map/scores_backward/pallas_call | solution.py:579
  202.7 12.8 %ssd_backward.2 = (f32[1024,768]{1,0:T(8,128)}, bf16[1024,128]{1,0:T(8,128)(2,1)}, f32[8,768]{1,0:T(8,128)}, f32[48,768]{1,0:T(8,128)}, f32[16,128]{1,0:T(8,128)}) custom-call(bf16[1024,1024]{1,0:T(8,128)(2,1)} %get-tuple-element.65.xa_ref.bm_ref.cm_ref.cm, bf16[1024,1024]{1,0:T(8,128)(2,1)} %get-tuple-element.65.xa_ref.bm_ref.cm_ref.cm, ...), custom_call_target="tpu_custom_call" | custom-call | flops 805306368 | bytes 9437184 | tf_op jit(solution)/shard_map/ssd_backward/pallas_call | solution.py:735
  215.7 21.2 %ssd_backward.3 = (f32[1024,768]{1,0:T(8,128)}, bf16[1024,128]{1,0:T(8,128)(2,1)}, f32[8,768]{1,0:T(8,128)}, f32[48,768]{1,0:T(8,128)}, f32[16,128]{1,0:T(8,128)}) custom-call(bf16[1024,1024]{1,0:T(8,128)(2,1)} %get-tuple-element.65.xa_ref.bm_ref.cm_ref.cm, ...), custom_call_target="tpu_custom_call", output_to_operand_aliasing={{0}: (18, {}), {1}: (19, {})} | custom-call | flops 805306368 | bytes 9437184 | tf_op jit(solution)/shard_map/ssd_backward/pallas_call | solution.py:735
  239.0 2.7 collective-permute-start.51
  245.9 3.8 collective-permute-done.24
  250.6 2.5 bc_backward.1
  256.5 2.5 collective-permute-start.53
  260.0 14.1 %input_stage.1 = (bf16[512,1536]{1,0:T(8,128)(2,1)}, bf16[512,1536]{1,0:T(8,128)(2,1)}, bf16[1024,512]{1,0:T(8,128)(2,1)}, bf16[1024,384]{1,0:T(8,128)(2,1)}) custom-call(s32[2]{0:T(128)} %pad_add_fusion.place.where, f32[1024,768]{1,0:T(8,128)} %get-tuple-element.96.gx_ref.gx_next, f32[1024,768]{1,0:T(8,128)} %get-tuple-element.96.gx_ref.gx_next, ...), custom_call_target="tpu_custom_call" | custom-call | flops 4831838208 | bytes 11010048 | tf_op jit(solution)/shard_map/input_stage/pallas_call | solution.py:846
  274.1 5.2 %late_grads.3 = (bf16[4,192,384]{2,1,0:T(8,128)(2,1)}, bf16[4,192,384]{2,1,0:T(8,128)(2,1)}) custom-call(s32[1]{0:T(128)} %bitcast.26.side, bf16[1536,1024]{1,0:T(8,128)(2,1)} %fusion.38.normed_t, bf16[1024,384]{1,0:T(8,128)(2,1)} %get-tuple-element.107.gcat), custom_call_target="tpu_custom_call" | custom-call | flops 1207959552 | bytes 5111808 | tf_op jit(solution)/shard_map/late_grads/pallas_call | solution.py:902
  281.9 5.4 %late_grads.2 = (bf16[4,192,512]{2,1,0:T(8,128)(2,1)}, bf16[4,192,512]{2,1,0:T(8,128)(2,1)}) custom-call(s32[1]{0:T(128)} %bitcast.26.side, bf16[1536,1024]{1,0:T(8,128)(2,1)} %fusion.38.normed_t, bf16[1024,512]{1,0:T(8,128)(2,1)} %get-tuple-element.104.gcat), custom_call_target="tpu_custom_call" | custom-call | flops 1610612736 | bytes 5767168 | tf_op jit(solution)/shard_map/late_grads/pallas_call | solution.py:902
  287.9 13.7 %collective-permute-done.43 = bf16[4,192,384]{2,1,0:T(8,128)(2,1)S(1)} collective-permute-done((bf16[4,192,384]{2,1,0:T(8,128)(2,1)}, bf16[4,192,384]{2,1,0:T(8,128)(2,1)S(1)}, u32[]{:S(2)}, u32[]{:S(2)}) %collective-permute-start.43) | collective-permute-done | bytes 589856 | tf_op jit(solution)/shard_map/ppermute | solution.py:75
  304.4 3.4 collective-permute-start.44
  311.2 4.2 collective-permute-start.45
  315.4 3.0 collective-permute-done.36
  326.3 3.4 collective-permute-start.37
  334.9 11.3 %collective-permute-start.38 = (bf16[192,512]{1,0:T(8,128)(2,1)S(1)}, bf16[192,512]{1,0:T(8,128)(2,1)}, u32[]{:S(2)}, u32[]{:S(2)}) collective-permute-start(bf16[192,512]{1,0:T(8,128)(2,1)S(1)} %fusion.14), channel_id=1, source_target_pairs={{0,8},{8,16},{1,9},{9,17},{2,10},{10,18},{3,11},{11,19},{4,12},{12... | collective-permute-start | bytes 589832 | tf_op jit(solution)/shard_map/ppermute | solution.py:84
  348.5 9.3 %collective-permute-done.27 = bf16[256,1536]{1,0:T(8,128)(2,1)S(1)} collective-permute-done((bf16[256,1536]{1,0:T(8,128)(2,1)S(1)}, bf16[256,1536]{1,0:T(8,128)(2,1)S(1)}, u32[]{:S(2)}, u32[]{:S(2)}) %collective-permute-start.27) | collective-permute-done | bytes 786464 | tf_op jit(solution)/shard_map/ppermute | solution.py:97
  357.8 4.2 fusion.9
  365.5 3.5 fusion.6.own
  374.6 32.1 %collective-permute-done.32 = f32[22,256]{1,0:T(8,128)S(1)} collective-permute-done((f32[22,256]{1,0:T(8,128)S(1)}, f32[22,256]{1,0:T(8,128)S(1)}, u32[]{:S(2)}, u32[]{:S(2)}) %collective-permute-start.32) | collective-permute-done | bytes 22560 | tf_op jit(solution)/shard_map/ppermute | solution.py:28
  406.6 3.4 collective-permute-start.39
  415.7 2.7 collective-permute-done.42
  419.5 2.7 collective-permute-done.34
  422.2 2.2 collective-permute-start.35
  424.5 2.5 collective-permute-done.35
  430.2 4.7 %assemble.2 = bf16[1024,1536]{1,0:T(8,128)(2,1)} custom-call(s32[2]{0:T(128)} %pad_add_fusion.place.where, bf16[256,1536]{1,0:T(8,128)(2,1)} %get-tuple-element.153.own, bf16[256,1536]{1,0:T(8,128)(2,1)} %copy-done.18, bf16[256,1536]{1,0:T(8,128)(2,1)} %collective-permute-done.19.core_a, bf16[256,1536]{1,0:T(8,128)(2,1)} %collective-permute-done.20.core_b), custom_call_target="tpu_custom_call" | custom-call | bytes 4718592 | tf_op jit(solution)/shard_map/assemble/pallas_call | solution.py:116
  435.7 5.6 %assemble.3 = f32[1024,1536]{1,0:T(8,128)} custom-call(s32[2]{0:T(128)} %pad_add_fusion.place.where, bf16[256,1536]{1,0:T(8,128)(2,1)} %fusion.6.own, bf16[256,1536]{1,0:T(8,128)(2,1)} %copy-done.17, bf16[256,1536]{1,0:T(8,128)(2,1)} %copy-done.19, bf16[256,1536]{1,0:T(8,128)(2,1)} %collective-permute-done.30.core_b), custom_call_target="tpu_custom_call" | custom-call | bytes 4718592 | tf_op jit(solution)/shard_map/assemble/pallas_call | solution.py:116
  (287 shorter events, 102.3 us)
Async XLA Ops:
  7.2 131.9 %all-gather.2.cloned.1.call-start = ((), (), s32[]{:S(2)}) async-start(), calls=%async_computation.1 | async-start | bytes 5308416 | tf_op jit(solution)/shard_map/all_gather | solution.py:959
  11.3 430.0 %reduce-scatter.2.cloned.1.call-start = ((), (), s32[]{:S(2)}) async-start(), calls=%async_computation.2 | async-start | bytes 5308416 | tf_op jit(solution)/shard_map/reduce_scatter | solution.py:1000
  13.4 30.7 %collective-permute-start.2 = (bf16[192,1152]{1,0:T(8,128)(2,1)}, bf16[192,1152]{1,0:T(8,128)(2,1)}, u32[]{:S(2)}, u32[]{:S(2)}) collective-permute-start(bf16[192,1152]{1,0:T(8,128)(2,1)} %constant_dynamic-slice_fusion), channel_id=1, source_target_pairs={{8,0},{12,4},{16,8},{20,12},{24,16},{28,20},{9,1},{13,5},{17,9},{2... | collective-permute-start | bytes 1327112 | tf_op jit(solution)/shard_map/ppermute | solution.py:62
  14.7 32.7 %collective-permute-start.1 = (bf16[192,1152]{1,0:T(8,128)(2,1)}, bf16[192,1152]{1,0:T(8,128)(2,1)}, u32[]{:S(2)}, u32[]{:S(2)}) collective-permute-start(bf16[192,1152]{1,0:T(8,128)(2,1)} %constant_dynamic-slice_fusion), channel_id=1, source_target_pairs={{0,8},{4,12},{8,16},{12,20},{16,24},{20,28},{1,9},{5,13},{9,17},{1... | collective-permute-start | bytes 1327112 | tf_op jit(solution)/shard_map/ppermute | solution.py:61
  21.9 21.5 %collective-permute-start = (bf16[8,1536]{1,0:T(8,128)(2,1)S(1)}, bf16[8,1536]{1,0:T(8,128)(2,1)S(1)}, u32[]{:S(2)}, u32[]{:S(2)}) collective-permute-start(bf16[8,1536]{1,0:T(8,128)(2,1)S(1)} %slice_bitcast_fusion.2), channel_id=1, source_target_pairs={{0,4},{1,5},{2,6},{3,7},{8,12},{9,13},{10,14},{11,15},{16,20},{17,... | collective-permute-start | bytes 73736 | tf_op jit(solution)/shard_map/ppermute | solution.py:36
  44.1 13.4 %collective-permute-start.6 = (bf16[192,1152]{1,0:T(8,128)(2,1)}, bf16[192,1152]{1,0:T(8,128)(2,1)S(1)}, u32[]{:S(2)}, u32[]{:S(2)}) collective-permute-start(bf16[192,1152]{1,0:T(8,128)(2,1)} %collective-permute-done.2), channel_id=1, source_target_pairs={{8,0},{12,4},{16,8},{20,12},{9,1},{13,5},{17,9},{21,13},{10,2},{14... | collective-permute-start | bytes 1327112 | tf_op jit(solution)/shard_map/ppermute | solution.py:62
  45.4 18.8 %collective-permute-start.4 = (bf16[192,1152]{1,0:T(8,128)(2,1)}, bf16[192,1152]{1,0:T(8,128)(2,1)S(1)}, u32[]{:S(2)}, u32[]{:S(2)}) collective-permute-start(bf16[192,1152]{1,0:T(8,128)(2,1)} %collective-permute-done.2), channel_id=1, source_target_pairs={{0,4},{4,0},{8,12},{12,8},{16,20},{20,16},{1,5},{5,1},{9,13},{13,9... | collective-permute-start | bytes 1327112 | tf_op jit(solution)/shard_map/ppermute | solution.py:64
  47.4 14.7 %collective-permute-start.5 = (bf16[192,1152]{1,0:T(8,128)(2,1)}, bf16[192,1152]{1,0:T(8,128)(2,1)S(1)}, u32[]{:S(2)}, u32[]{:S(2)}) collective-permute-start(bf16[192,1152]{1,0:T(8,128)(2,1)} %collective-permute-done.1), channel_id=1, source_target_pairs={{8,16},{12,20},{16,24},{20,28},{9,17},{13,21},{17,25},{21,29},{10,... | collective-permute-start | bytes 1327112 | tf_op jit(solution)/shard_map/ppermute | solution.py:61
  48.1 14.7 %collective-permute-start.3 = (bf16[192,1152]{1,0:T(8,128)(2,1)}, bf16[192,1152]{1,0:T(8,128)(2,1)S(1)}, u32[]{:S(2)}, u32[]{:S(2)}) collective-permute-start(bf16[192,1152]{1,0:T(8,128)(2,1)} %collective-permute-done.1), channel_id=1, source_target_pairs={{8,12},{12,8},{16,20},{20,16},{24,28},{28,24},{9,13},{13,9},{17,21... | collective-permute-start | bytes 1327112 | tf_op jit(solution)/shard_map/ppermute | solution.py:63
  57.6 33.9 %collective-permute-start.10 = (bf16[192,1152]{1,0:T(8,128)(2,1)S(1)}, bf16[192,1152]{1,0:T(8,128)(2,1)S(1)}, u32[]{:S(2)}, u32[]{:S(2)}) collective-permute-start(bf16[192,1152]{1,0:T(8,128)(2,1)S(1)} %collective-permute-done.6), channel_id=1, source_target_pairs={{8,0},{12,4},{9,1},{13,5},{10,2},{14,6},{11,3},{15,7}} | collective-permute-start | bytes 1327112 | tf_op jit(solution)/shard_map/ppermute | solution.py:62
  58.8 37.4 %collective-permute-start.8 = (bf16[192,1152]{1,0:T(8,128)(2,1)S(1)}, bf16[192,1152]{1,0:T(8,128)(2,1)S(1)}, u32[]{:S(2)}, u32[]{:S(2)}) collective-permute-start(bf16[192,1152]{1,0:T(8,128)(2,1)S(1)} %collective-permute-done.6), channel_id=1, source_target_pairs={{0,4},{4,0},{8,12},{12,8},{1,5},{5,1},{9,13},{13,9},{2,6},{6,2},{1... | collective-permute-start | bytes 1327112 | tf_op jit(solution)/shard_map/ppermute | solution.py:64
  62.0 32.7 %collective-permute-start.9 = (bf16[192,1152]{1,0:T(8,128)(2,1)S(1)}, bf16[192,1152]{1,0:T(8,128)(2,1)S(1)}, u32[]{:S(2)}, u32[]{:S(2)}) collective-permute-start(bf16[192,1152]{1,0:T(8,128)(2,1)S(1)} %collective-permute-done.5), channel_id=1, source_target_pairs={{16,24},{20,28},{17,25},{21,29},{18,26},{22,30},{19,27},{23,31}} | collective-permute-start | bytes 1327112 | tf_op jit(solution)/shard_map/ppermute | solution.py:61
  62.7 32.7 %collective-permute-start.7 = (bf16[192,1152]{1,0:T(8,128)(2,1)S(1)}, bf16[192,1152]{1,0:T(8,128)(2,1)S(1)}, u32[]{:S(2)}, u32[]{:S(2)}) collective-permute-start(bf16[192,1152]{1,0:T(8,128)(2,1)S(1)} %collective-permute-done.5), channel_id=1, source_target_pairs={{16,20},{20,16},{24,28},{28,24},{17,21},{21,17},{25,29},{29,25},{1... | collective-permute-start | bytes 1327112 | tf_op jit(solution)/shard_map/ppermute | solution.py:63
  91.4 13.2 %collective-permute-start.12 = (bf16[192,1152]{1,0:T(8,128)(2,1)S(1)}, bf16[192,1152]{1,0:T(8,128)(2,1)S(1)}, u32[]{:S(2)}, u32[]{:S(2)}) collective-permute-start(bf16[192,1152]{1,0:T(8,128)(2,1)S(1)} %collective-permute-done.10), channel_id=1, source_target_pairs={{0,4},{4,0},{1,5},{5,1},{2,6},{6,2},{3,7},{7,3}} | collective-permute-start | bytes 1327112 | tf_op jit(solution)/shard_map/ppermute | solution.py:64
  132.2 6.8 %collective-permute-start.13 = (bf16[128,768]{1,0:T(8,128)(2,1)S(1)}, bf16[128,768]{1,0:T(8,128)(2,1)S(1)}, u32[]{:S(2)}, u32[]{:S(2)}) collective-permute-start(bf16[128,768]{1,0:T(8,128)(2,1)S(1)} %convert_element_type.262), channel_id=1, source_target_pairs={{0,4},{1,5},{2,6},{3,7},{8,12},{9,13},{10,14},{11,15},{16,20},{17,... | collective-permute-start | bytes 589832 | tf_op jit(solution)/shard_map/ppermute | solution.py:36
  155.3 8.2 %collective-permute-start.15 = (f32[8,1024]{1,0:T(8,128)S(1)}, f32[8,1024]{1,0:T(8,128)S(1)}, u32[]{:S(2)}, u32[]{:S(2)}) collective-permute-start(f32[8,1024]{1,0:T(8,128)S(1)} %add.356), channel_id=1, source_target_pairs={{0,2},{1,3},{2,0},{3,1},{4,6},{5,7},{6,4},{7,5},{8,10},{9,11},{10,... | collective-permute-start | bytes 98312 | tf_op jit(solution)/shard_map/ppermute | solution.py:28
  178.0 10.8 %collective-permute-start.21 = (bf16[128,768]{1,0:T(8,128)(2,1)}, bf16[128,768]{1,0:T(8,128)(2,1)S(1)}, u32[]{:S(2)}, u32[]{:S(2)}) collective-permute-start(bf16[128,768]{1,0:T(8,128)(2,1)} %get-tuple-element.79), channel_id=1, source_target_pairs={{4,0},{5,1},{6,2},{7,3},{12,8},{13,9},{14,10},{15,11},{20,16},{21,... | collective-permute-start | bytes 589832 | tf_op jit(solution)/shard_map/ppermute | solution.py:36
  201.9 13.6 %collective-permute-start.22 = (bf16[1024,128]{1,0:T(8,128)(2,1)S(1)}, bf16[1024,128]{1,0:T(8,128)(2,1)S(1)}, u32[]{:S(2)}, u32[]{:S(2)}) collective-permute-start(bf16[1024,128]{1,0:T(8,128)(2,1)S(1)} %broadcast_select_fusion), channel_id=1, source_target_pairs={{0,1},{1,0},{2,3},{3,2},{4,5},{5,4},{6,7},{7,6},{8,9},{9,8},{10,11... | collective-permute-start | bytes 786440 | tf_op jit(solution)/shard_map/ppermute | solution.py:1015
  239.0 6.8 %collective-permute-start.51 = (f32[41,768]{1,0:T(8,128)S(1)}, f32[41,768]{1,0:T(8,128)S(1)}, u32[]{:S(2)}, u32[]{:S(2)}) collective-permute-start(f32[41,768]{1,0:T(8,128)S(1)} %select_maximum_fusion), channel_id=1, source_target_pairs={{0,4},{4,0},{1,5},{5,1},{2,6},{6,2},{3,7},{7,3},{8,12},{12,8},{9,1... | collective-permute-start | bytes 377864 | tf_op jit(solution)/shard_map/ppermute | solution.py:28
  241.7 8.0 %collective-permute-start.24 = (bf16[1024,128]{1,0:T(8,128)(2,1)S(1)}, bf16[1024,128]{1,0:T(8,128)(2,1)S(1)}, u32[]{:S(2)}, u32[]{:S(2)}) collective-permute-start(bf16[1024,128]{1,0:T(8,128)(2,1)S(1)} %add_convert_fusion.4), channel_id=1, source_target_pairs={{0,2},{1,3},{2,0},{3,1},{4,6},{5,7},{6,4},{7,5},{8,10},{9,11},{10,... | collective-permute-start | bytes 786440 | tf_op jit(solution)/shard_map/ppermute | solution.py:1021
  243.7 15.4 %collective-permute-start.23 = (f32[8,768]{1,0:T(8,128)S(1)}, f32[8,768]{1,0:T(8,128)S(1)}, u32[]{:S(2)}, u32[]{:S(2)}) collective-permute-start(f32[8,768]{1,0:T(8,128)S(1)} %copy-done.43), channel_id=1, source_target_pairs={{4,0},{5,1},{6,2},{7,3},{12,8},{13,9},{14,10},{15,11},{20,16},{21,... | collective-permute-start | bytes 73736 | tf_op jit(solution)/shard_map/ppermute | solution.py:36
  245.9 10.7 %collective-permute-start.52 = (f32[41,768]{1,0:T(8,128)S(1)}, f32[41,768]{1,0:T(8,128)S(1)}, u32[]{:S(2)}, u32[]{:S(2)}) collective-permute-start(f32[41,768]{1,0:T(8,128)S(1)} %fusion.34), channel_id=1, source_target_pairs={{0,8},{8,0},{16,24},{24,16},{1,9},{9,1},{17,25},{25,17},{2,10},{10... | collective-permute-start | bytes 377864 | tf_op jit(solution)/shard_map/ppermute | solution.py:28
  255.7 64.1 %collective-permute-start.16 = (bf16[512,1536]{1,0:T(8,128)(2,1)}, bf16[512,1536]{1,0:T(8,128)(2,1)}, u32[]{:S(2)}, u32[]{:S(2)}) collective-permute-start(bf16[512,1536]{1,0:T(8,128)(2,1)} %get-tuple-element.77), channel_id=1, source_target_pairs={{0,1},{1,0},{2,3},{3,2},{4,5},{5,4},{6,7},{7,6},{8,9},{9,8},{10,11... | collective-permute-start | bytes 4718600 | tf_op jit(solution)/shard_map/ppermute | solution.py:94
  256.5 30.8 %collective-permute-start.53 = (f32[41,768]{1,0:T(8,128)S(1)}, f32[41,768]{1,0:T(8,128)S(1)}, u32[]{:S(2)}, u32[]{:S(2)}) collective-permute-start(f32[41,768]{1,0:T(8,128)S(1)} %add.392), channel_id=1, source_target_pairs={{0,16},{8,24},{16,0},{24,8},{1,17},{9,25},{17,1},{25,9},{2,18},{10... | collective-permute-start | bytes 377864 | tf_op jit(solution)/shard_map/ppermute | solution.py:28
  279.2 22.3 %collective-permute-start.43 = (bf16[4,192,384]{2,1,0:T(8,128)(2,1)}, bf16[4,192,384]{2,1,0:T(8,128)(2,1)S(1)}, u32[]{:S(2)}, u32[]{:S(2)}) collective-permute-start(bf16[4,192,384]{2,1,0:T(8,128)(2,1)} %get-tuple-element.109), channel_id=1, source_target_pairs={{0,4},{4,0},{1,5},{5,1},{2,6},{6,2},{3,7},{7,3},{8,12},{12,8},{9,1... | collective-permute-start | bytes 1769480 | tf_op jit(solution)/shard_map/ppermute | solution.py:75
  287.2 31.2 %collective-permute-start.36 = (bf16[4,192,512]{2,1,0:T(8,128)(2,1)}, bf16[4,192,512]{2,1,0:T(8,128)(2,1)}, u32[]{:S(2)}, u32[]{:S(2)}) collective-permute-start(bf16[4,192,512]{2,1,0:T(8,128)(2,1)} %get-tuple-element.106), channel_id=1, source_target_pairs={{0,4},{4,0},{1,5},{5,1},{2,6},{6,2},{3,7},{7,3},{8,12},{12,8},{9,1... | collective-permute-start | bytes 2359304 | tf_op jit(solution)/shard_map/ppermute | solution.py:75
  287.4 34.9 %collective-permute-start.26 = (bf16[512,1536]{1,0:T(8,128)(2,1)}, bf16[512,1536]{1,0:T(8,128)(2,1)S(1)}, u32[]{:S(2)}, u32[]{:S(2)}) collective-permute-start(bf16[512,1536]{1,0:T(8,128)(2,1)} %get-tuple-element.102), channel_id=1, source_target_pairs={{0,1},{1,0},{2,3},{3,2},{4,5},{5,4},{6,7},{7,6},{8,9},{9,8},{10,11... | collective-permute-start | bytes 4718600 | tf_op jit(solution)/shard_map/ppermute | solution.py:94
  310.5 19.2 %collective-permute-start.47 = (bf16[192,384]{1,0:T(8,128)(2,1)}, bf16[192,384]{1,0:T(8,128)(2,1)S(1)}, u32[]{:S(2)}, u32[]{:S(2)}) collective-permute-start(bf16[192,384]{1,0:T(8,128)(2,1)} %get-tuple-element.165), channel_id=1, source_target_pairs={{24,16},{25,17},{26,18},{27,19},{28,20},{29,21},{30,22},{31,23}} | collective-permute-start | bytes 442376 | tf_op jit(solution)/shard_map/ppermute | solution.py:85
  311.2 19.8 %collective-permute-start.45 = (bf16[192,384]{1,0:T(8,128)(2,1)S(1)}, bf16[192,384]{1,0:T(8,128)(2,1)S(1)}, u32[]{:S(2)}, u32[]{:S(2)}) collective-permute-start(bf16[192,384]{1,0:T(8,128)(2,1)S(1)} %fusion.20), channel_id=1, source_target_pairs={{0,8},{8,16},{1,9},{9,17},{2,10},{10,18},{3,11},{11,19},{4,12},{12... | collective-permute-start | bytes 442376 | tf_op jit(solution)/shard_map/ppermute | solution.py:84
  321.5 25.5 %collective-permute-start.17 = (bf16[256,1536]{1,0:T(8,128)(2,1)S(1)}, bf16[256,1536]{1,0:T(8,128)(2,1)S(1)}, u32[]{:S(2)}, u32[]{:S(2)}) collective-permute-start(bf16[256,1536]{1,0:T(8,128)(2,1)S(1)} %add_convert_fusion.2), channel_id=1, source_target_pairs={{0,2},{1,3},{2,0},{3,1},{4,6},{5,7},{6,4},{7,5},{8,10},{9,11},{10,... | collective-permute-start | bytes 2359304 | tf_op jit(solution)/shard_map/ppermute | solution.py:97
  324.9 33.0 %collective-permute-start.27 = (bf16[256,1536]{1,0:T(8,128)(2,1)S(1)}, bf16[256,1536]{1,0:T(8,128)(2,1)S(1)}, u32[]{:S(2)}, u32[]{:S(2)}) collective-permute-start(bf16[256,1536]{1,0:T(8,128)(2,1)S(1)} %add_convert_fusion.1), channel_id=1, source_target_pairs={{0,2},{1,3},{2,0},{3,1},{4,6},{5,7},{6,4},{7,5},{8,10},{9,11},{10,... | collective-permute-start | bytes 2359304 | tf_op jit(solution)/shard_map/ppermute | solution.py:97
  326.3 7.9 %collective-permute-start.37 = (bf16[192,512]{1,0:T(8,128)(2,1)S(1)}, bf16[192,512]{1,0:T(8,128)(2,1)S(1)}, u32[]{:S(2)}, u32[]{:S(2)}) collective-permute-start(bf16[192,512]{1,0:T(8,128)(2,1)S(1)} %get-tuple-element.160), channel_id=1, source_target_pairs={{0,8},{1,9},{2,10},{3,11},{4,12},{5,13},{6,14},{7,15}} | collective-permute-start | bytes 589832 | tf_op jit(solution)/shard_map/ppermute | solution.py:84
  329.7 39.4 %collective-permute-start.40 = (bf16[192,512]{1,0:T(8,128)(2,1)S(1)}, bf16[192,512]{1,0:T(8,128)(2,1)}, u32[]{:S(2)}, u32[]{:S(2)}) collective-permute-start(bf16[192,512]{1,0:T(8,128)(2,1)S(1)} %get-tuple-element.161), channel_id=1, source_target_pairs={{24,16},{25,17},{26,18},{27,19},{28,20},{29,21},{30,22},{31,23}} | collective-permute-start | bytes 589832 | tf_op jit(solution)/shard_map/ppermute | solution.py:85
  331.8 41.2 %collective-permute-start.46 = (bf16[192,384]{1,0:T(8,128)(2,1)}, bf16[192,384]{1,0:T(8,128)(2,1)}, u32[]{:S(2)}, u32[]{:S(2)}) collective-permute-start(bf16[192,384]{1,0:T(8,128)(2,1)} %get-tuple-element.162), channel_id=1, source_target_pairs={{0,8},{8,16},{16,24},{1,9},{9,17},{17,25},{2,10},{10,18},{18,26},{... | collective-permute-start | bytes 442376 | tf_op jit(solution)/shard_map/ppermute | solution.py:84
  334.9 34.5 %collective-permute-start.38 = (bf16[192,512]{1,0:T(8,128)(2,1)S(1)}, bf16[192,512]{1,0:T(8,128)(2,1)}, u32[]{:S(2)}, u32[]{:S(2)}) collective-permute-start(bf16[192,512]{1,0:T(8,128)(2,1)S(1)} %fusion.14), channel_id=1, source_target_pairs={{0,8},{8,16},{1,9},{9,17},{2,10},{10,18},{3,11},{11,19},{4,12},{12... | collective-permute-start | bytes 589832 | tf_op jit(solution)/shard_map/ppermute | solution.py:84
  347.0 26.4 %collective-permute-start.49 = (bf16[192,384]{1,0:T(8,128)(2,1)}, bf16[192,384]{1,0:T(8,128)(2,1)}, u32[]{:S(2)}, u32[]{:S(2)}) collective-permute-start(bf16[192,384]{1,0:T(8,128)(2,1)} %fusion.19), channel_id=1, source_target_pairs={{24,16},{16,8},{8,0},{25,17},{17,9},{9,1},{26,18},{18,10},{10,2},{... | collective-permute-start | bytes 442376 | tf_op jit(solution)/shard_map/ppermute | solution.py:85
  364.8 7.5 %collective-permute-start.31 = (f32[22,256]{1,0:T(8,128)S(1)}, f32[22,256]{1,0:T(8,128)S(1)}, u32[]{:S(2)}, u32[]{:S(2)}) collective-permute-start(f32[22,256]{1,0:T(8,128)S(1)} %select_maximum_fusion.2), channel_id=1, source_target_pairs={{0,1},{1,0},{2,3},{3,2},{4,5},{5,4},{6,7},{7,6},{8,9},{9,8},{10,11... | collective-permute-start | bytes 67592 | tf_op jit(solution)/shard_map/ppermute | solution.py:28
  369.1 45.4 %collective-permute-start.28 = (bf16[256,1536]{1,0:T(8,128)(2,1)}, bf16[256,1536]{1,0:T(8,128)(2,1)S(1)}, u32[]{:S(2)}, u32[]{:S(2)}) collective-permute-start(bf16[256,1536]{1,0:T(8,128)(2,1)} %fusion.6.own), channel_id=1, source_target_pairs={{0,2},{1,3},{2,0},{3,1},{4,6},{5,7},{6,4},{7,5},{8,10},{9,11},{10,... | collective-permute-start | bytes 2359304 | tf_op jit(solution)/shard_map/ppermute | solution.py:111
  369.4 45.2 %collective-permute-start.18 = (bf16[256,1536]{1,0:T(8,128)(2,1)}, bf16[256,1536]{1,0:T(8,128)(2,1)S(1)}, u32[]{:S(2)}, u32[]{:S(2)}) collective-permute-start(bf16[256,1536]{1,0:T(8,128)(2,1)} %get-tuple-element.153.own), channel_id=1, source_target_pairs={{0,2},{1,3},{2,0},{3,1},{4,6},{5,7},{6,4},{7,5},{8,10},{9,11},{10,... | collective-permute-start | bytes 2359304 | tf_op jit(solution)/shard_map/ppermute | solution.py:111
  372.2 37.8 %collective-permute-start.41 = (bf16[192,512]{1,0:T(8,128)(2,1)S(1)}, bf16[192,512]{1,0:T(8,128)(2,1)S(1)}, u32[]{:S(2)}, u32[]{:S(2)}) collective-permute-start(bf16[192,512]{1,0:T(8,128)(2,1)S(1)} %get-tuple-element.159), channel_id=1, source_target_pairs={{24,16},{16,8},{25,17},{17,9},{26,18},{18,10},{27,19},{19,11},{28,... | collective-permute-start | bytes 589832 | tf_op jit(solution)/shard_map/ppermute | solution.py:85
  373.0 33.6 %collective-permute-start.32 = (f32[22,256]{1,0:T(8,128)S(1)}, f32[22,256]{1,0:T(8,128)S(1)}, u32[]{:S(2)}, u32[]{:S(2)}) collective-permute-start(f32[22,256]{1,0:T(8,128)S(1)} %fusion.33), channel_id=1, source_target_pairs={{0,2},{1,3},{2,0},{3,1},{4,6},{5,7},{6,4},{7,5},{8,10},{9,11},{10,... | collective-permute-start | bytes 67592 | tf_op jit(solution)/shard_map/ppermute | solution.py:28
  374.5 36.1 %collective-permute-start.50 = (f32[192,128]{1,0:T(8,128)S(1)}, f32[192,128]{1,0:T(8,128)S(1)}, u32[]{:S(2)}, u32[]{:S(2)}) collective-permute-start(f32[192,128]{1,0:T(8,128)S(1)} %slice.139), channel_id=1, source_target_pairs={{0,1},{1,0},{2,3},{3,2},{4,5},{5,4},{6,7},{7,6},{8,9},{9,8},{10,11... | collective-permute-start | bytes 294920 | tf_op jit(solution)/shard_map/ppermute | solution.py:1090
  406.6 7.3 %collective-permute-start.39 = (bf16[192,512]{1,0:T(8,128)(2,1)S(1)}, bf16[192,512]{1,0:T(8,128)(2,1)S(1)}, u32[]{:S(2)}, u32[]{:S(2)}) collective-permute-start(bf16[192,512]{1,0:T(8,128)(2,1)S(1)} %get-tuple-element.158), channel_id=1, source_target_pairs={{0,8},{8,16},{16,24},{1,9},{9,17},{17,25},{2,10},{10,18},{18,26},{... | collective-permute-start | bytes 589832 | tf_op jit(solution)/shard_map/ppermute | solution.py:84
  410.6 7.8 %collective-permute-start.42 = (bf16[192,512]{1,0:T(8,128)(2,1)S(1)}, bf16[192,512]{1,0:T(8,128)(2,1)S(1)}, u32[]{:S(2)}, u32[]{:S(2)}) collective-permute-start(bf16[192,512]{1,0:T(8,128)(2,1)S(1)} %fusion.13), channel_id=1, source_target_pairs={{24,16},{16,8},{8,0},{25,17},{17,9},{9,1},{26,18},{18,10},{10,2},{... | collective-permute-start | bytes 589832 | tf_op jit(solution)/shard_map/ppermute | solution.py:85
  413.9 20.9 %collective-permute-start.29 = (bf16[256,1536]{1,0:T(8,128)(2,1)}, bf16[256,1536]{1,0:T(8,128)(2,1)S(1)}, u32[]{:S(2)}, u32[]{:S(2)}) collective-permute-start(bf16[256,1536]{1,0:T(8,128)(2,1)} %fusion.6.own), channel_id=1, source_target_pairs={{0,1},{1,0},{2,3},{3,2},{4,5},{5,4},{6,7},{7,6},{8,9},{9,8},{10,11... | collective-permute-start | bytes 2359304 | tf_op jit(solution)/shard_map/ppermute | solution.py:112
  413.9 16.2 %collective-permute-start.19 = (bf16[256,1536]{1,0:T(8,128)(2,1)}, bf16[256,1536]{1,0:T(8,128)(2,1)}, u32[]{:S(2)}, u32[]{:S(2)}) collective-permute-start(bf16[256,1536]{1,0:T(8,128)(2,1)} %get-tuple-element.153.own), channel_id=1, source_target_pairs={{0,1},{1,0},{2,3},{3,2},{4,5},{5,4},{6,7},{7,6},{8,9},{9,8},{10,11... | collective-permute-start | bytes 2359304 | tf_op jit(solution)/shard_map/ppermute | solution.py:112
  414.5 20.4 %collective-permute-start.30 = (bf16[256,1536]{1,0:T(8,128)(2,1)S(1)}, bf16[256,1536]{1,0:T(8,128)(2,1)}, u32[]{:S(2)}, u32[]{:S(2)}) collective-permute-start(bf16[256,1536]{1,0:T(8,128)(2,1)S(1)} %collective-permute-done.28.chip), channel_id=1, source_target_pairs={{0,1},{1,0},{2,3},{3,2},{4,5},{5,4},{6,7},{7,6},{8,9},{9,8},{10,11... | collective-permute-start | bytes 2359304 | tf_op jit(solution)/shard_map/ppermute | solution.py:113
  414.5 15.6 %collective-permute-start.20 = (bf16[256,1536]{1,0:T(8,128)(2,1)S(1)}, bf16[256,1536]{1,0:T(8,128)(2,1)}, u32[]{:S(2)}, u32[]{:S(2)}) collective-permute-start(bf16[256,1536]{1,0:T(8,128)(2,1)S(1)} %collective-permute-done.18.chip), channel_id=1, source_target_pairs={{0,1},{1,0},{2,3},{3,2},{4,5},{5,4},{6,7},{7,6},{8,9},{9,8},{10,11... | collective-permute-start | bytes 2359304 | tf_op jit(solution)/shard_map/ppermute | solution.py:113
  (54 other events, 483.3 us)
Sparse Core Ops, SparseCore 0:
  11.4 108.1 all-gather.1
  202.4 104.8 reduce-scatter.1
